TPU v7x, 32 devices: a whole 2x2x4 slice. The times are simulated.
32 devices in a mesh: dp: 8 (over z, y), expert: 4 (over x, core).
Axes of the slice: x: 2, y: 2, z: 4, core: 2. Of those that a mesh axis runs over, the one named last changes fastest.
Arguments:
- tokens: bfloat16 [1024, 3072], P('expert'), may hold values from -6 to 6
- cotangent: bfloat16 [1024, 3072], P('expert'), may hold values from -6 to 6
- routes: int32 [1024, 2], P('expert'), may hold values from 0 to 3, all different within a row; in each aligned block of 256 rows (0 to 255, 256 to 511, ...) at most 128 rows name the same one
- gate_values: bfloat16 [1024, 2], P('expert'), may hold values from 0.049804688 to 0.94921875
- gate_weight: bfloat16 [4, 3072, 8192], P('expert', None, 'dp'), may hold values from -0.109375 to 0.109375
- up_weight: bfloat16 [4, 3072, 8192], P('expert', None, 'dp'), may hold values from -0.109375 to 0.109375
- down_weight: bfloat16 [4, 3072, 8192], P('expert', None, 'dp'), may hold values from -0.0625 to 0.0625
Outputs:
- clipped: bfloat16 [4, 3, 3072, 8192], P('expert', None, 'dp')
- d_tokens: bfloat16 [3072, 1024], P('dp', 'expert')
Inputs may be any that keep to these rules, and one draw needn't show every extreme that they name: `routes`: each row names two different experts. Within the 256 rows of one device along expert (aligned blocks), no expert is named by more than 128 rows.
All inputs are finite; a program needn't handle non-finite values.
Results may differ from a plain program's by a relative error of at most 0.0064.
Values may be sent and summed in bfloat16 or wider, within the bound.
No kernel may reach another device: no remote copies, remote signals or barrier semaphores. Data moves between devices by JAX's collectives and lax.ppermute only.
A program may use at most 128 MiB of HBM per device.

v0:
```python
import functools
import math

import jax
import jax.numpy as jnp
from jax import lax
from jax.experimental import pallas as pl
from jax.experimental.pallas import tpu as pltpu
from jax.sharding import PartitionSpec as P


CAP = 128
CLIP_RMS = 0.2
VMEM = 67043328


F32 = jnp.float32
BF16 = jnp.bfloat16


def tile_of(size, largest, unit):
    best = size
    for tile in range(unit, min(size, largest) + 1, unit):
        if size % tile == 0:
            best = tile
    return best


def params(dims=1):
    return pltpu.CompilerParams(
        dimension_semantics=("arbitrary",) * dims, vmem_limit_bytes=VMEM
    )


def dot_nn(left, right):
    return lax.dot_general(left, right, (((1,), (0,)), ((), ())), preferred_element_type=F32)


def dot_nt(left, right):
    return lax.dot_general(left, right, (((1,), (1,)), ((), ())), preferred_element_type=F32)


def dot_tn(left, right):
    return lax.dot_general(left, right, (((0,), (0,)), ((), ())), preferred_element_type=F32)


free = pl.BlockSpec(memory_space=pl.ANY)


def planes(refs, splits, plane):
    tiles, at = [], 0
    for count in splits:
        pieces = [ref[plane] for ref in refs[at : at + count]]
        tiles.append(pieces[0] if count == 1 else jnp.concatenate(pieces, axis=1))
        at += count
    return tiles[0] if len(tiles) == 1 else jnp.concatenate(tiles, axis=0)


def flat(parts):
    return [piece for part in parts for piece in part]


def held(values):
    return [pl.BlockSpec(value.shape, lambda *_: (0, 0, 0)) for value in values]


def stacked(refs):
    tiles = [ref[...] for ref in refs]
    return tiles[0] if len(tiles) == 1 else jnp.concatenate(tiles, axis=0)


def route_tiles(me, route_ref, gate_ref, pick_refs, gate_col, tiles):
    count = route_ref.shape[1]
    first, second = route_ref[0:1, :], route_ref[1:2, :]
    gates = gate_ref[...].astype(F32)
    hits = [jnp.logical_or(first == (me ^ r), second == (me ^ r)).astype(F32) for r in tiles]
    pad = (-len(tiles)) % 8
    rows = jnp.concatenate(hits + [jnp.zeros((pad, count), F32)] * (pad > 0), axis=0)
    earlier = (
        lax.broadcasted_iota(jnp.int32, (count, count), 0)
        < lax.broadcasted_iota(jnp.int32, (count, count), 1)
    ).astype(F32)
    before = dot_nn(rows.astype(BF16), earlier.astype(BF16))
    slot = lax.broadcasted_iota(jnp.int32, (CAP, count), 0).astype(F32)
    for k, r in enumerate(tiles):
        match = jnp.logical_and(slot == before[k : k + 1, :], hits[k] > 0.5)
        pick = jnp.where(match, 1.0, 0.0)
        weight = jnp.where(first == (me ^ r), gates[0:1, :], gates[1:2, :])
        gate_col[k * CAP : (k + 1) * CAP, :] = jnp.broadcast_to(
            jnp.sum(pick * weight, axis=1, keepdims=True), (CAP, 128)
        )
        pick_refs[k][...] = pick.astype(BF16)


def fill_rows(pick_refs, gate_col, tok_ref, cot_ref, x_refs, w_refs):
    pick = stacked(pick_refs)
    rows = dot_nn(pick, tok_ref[...])
    scaled = dot_nn(pick, cot_ref[...]) * gate_col[:, 0:1]
    for k in range(len(x_refs)):
        part = slice(k * CAP, (k + 1) * CAP)
        x_refs[k][...] = rows[part].astype(BF16)
        w_refs[k][...] = scaled[part].astype(BF16)


def fill_tiles(ids, routes, gates, tokens, cotangent, tiles):
    count, width = tokens.shape
    number = len(tiles)
    tn = tile_of(width, 1536, 128)

    def body(ids_ref, route_ref, gate_ref, tok_ref, cot_ref, *refs):
        x_refs, w_refs = refs[:number], refs[number : 2 * number]
        pick_refs, gate_col = refs[2 * number : 3 * number], refs[3 * number]

        @pl.when(pl.program_id(0) == 0)
        def _():
            route_tiles(ids_ref[1], route_ref, gate_ref, pick_refs, gate_col, tiles)

        fill_rows(pick_refs, gate_col, tok_ref, cot_ref, x_refs, w_refs)

    whole = lambda shape: pl.BlockSpec(shape, lambda j, ids: (0, 0))
    cols = lambda rows: pl.BlockSpec((rows, tn), lambda j, ids: (0, j))
    out = pl.pallas_call(
        body,
        out_shape=[jax.ShapeDtypeStruct((CAP, width), BF16)] * (2 * number)
        + [jax.ShapeDtypeStruct((CAP, count), BF16)] * number,
        grid_spec=pltpu.PrefetchScalarGridSpec(
            num_scalar_prefetch=1,
            grid=(width // tn,),
            in_specs=[whole((2, count)), whole((2, count)), cols(count), cols(count)],
            out_specs=[cols(CAP)] * (2 * number) + [whole((CAP, count))] * number,
            scratch_shapes=[pltpu.VMEM((number * CAP, 128), F32)],
        ),
        compiler_params=params(),
        cost_estimate=pl.CostEstimate(
            flops=4 * number * CAP * count * width,
            bytes_accessed=4 * (count + number * CAP) * width,
            transcendentals=0,
        ),
        name="fill",
    )(ids, routes, gates, tokens, cotangent)
    return out[:number], out[number : 2 * number], out[2 * number :]


def unit_values(x, w, gate_ref, up_ref, down_ref):
    pre_gate = dot_nn(x, gate_ref[...])
    pre_up = dot_nn(x, up_ref[...])
    grad_hidden = dot_nn(w, down_ref[...])
    sig = jax.nn.sigmoid(pre_gate)
    act = pre_gate * sig
    grad_gate = grad_hidden * pre_up * sig * (1.0 + pre_gate * (1.0 - sig))
    return (act * pre_up).astype(BF16), grad_gate.astype(BF16), (grad_hidden * act).astype(BF16)


def store_planes(out_ref, values):
    for k, value in enumerate(values):
        out_ref[k] = value


def first_units(routes, gates, tokens, cotangent, mats, tiles):
    count, width = tokens.shape
    units = mats[0].shape[1] // 2
    number = len(tiles)
    tn = tile_of(units, 256, 128)

    def body(route_ref, gates_ref, tok_ref, cot_ref, gate_ref, up_ref, down_ref, *refs):
        out_ref = refs[0]
        x_refs, w_refs = refs[1 : 1 + number], refs[1 + number : 1 + 2 * number]
        pick_refs, gate_col = refs[1 + 2 * number : 1 + 3 * number], refs[1 + 3 * number]

        @pl.when(pl.program_id(0) == 0)
        def _():
            me = lax.axis_index("expert")
            route_tiles(me, route_ref, gates_ref, pick_refs, gate_col, tiles)
            fill_rows(pick_refs, gate_col, tok_ref, cot_ref, x_refs, w_refs)

        values = unit_values(x_refs[0][...], w_refs[0][...], gate_ref, up_ref, down_ref)
        store_planes(out_ref, values)

    once = lambda shape: pl.BlockSpec(
        shape, lambda j: (0, 0), pipeline_mode=pl.Buffered(1)
    )
    whole = lambda shape: pl.BlockSpec(shape, lambda j: (0, 0))
    out = pl.pallas_call(
        body,
        out_shape=[jax.ShapeDtypeStruct((3, CAP, units), BF16)]
        + [jax.ShapeDtypeStruct((CAP, width), BF16)] * (2 * number)
        + [jax.ShapeDtypeStruct((CAP, count), BF16)] * number,
        grid_spec=pl.GridSpec(
            grid=(units // tn,),
            in_specs=[once((2, count)), once((2, count)), once((count, width)), once((count, width))]
            + [pl.BlockSpec((width, tn), lambda j: (0, j))] * 3,
            out_specs=[pl.BlockSpec((3, CAP, tn), lambda j: (0, 0, j))]
            + [whole((CAP, width))] * (2 * number)
            + [whole((CAP, count))] * number,
            scratch_shapes=[pltpu.VMEM((number * CAP, 128), F32)],
        ),
        compiler_params=params(),
        cost_estimate=pl.CostEstimate(
            flops=6 * CAP * width * units,
            bytes_accessed=2 * (3 * width * units + 2 * (count + number * CAP) * width),
            transcendentals=CAP * units,
        ),
        name="first",
    )(routes, gates, tokens, cotangent, *mats)
    return out[0], out[1 : 1 + number], out[1 + number : 1 + 2 * number], out[1 + 2 * number :]


def expert_units(x_tiles, w_tiles, mats, after, second_half=False):
    number = len(x_tiles)
    slots = number * CAP
    width, units = mats[0].shape
    half = units // 2
    tn = tile_of(half, 256, 128) if second_half else half
    skip = half // tn if second_half else 0
    outs = 1 if second_half else 2

    def body(*refs):
        x, w = stacked(refs[:number]), stacked(refs[number : 2 * number])
        gate_ref, up_ref, down_ref = refs[2 * number : 2 * number + 3]
        values = unit_values(x, w, gate_ref, up_ref, down_ref)
        if second_half:
            store_planes(refs[-1], values)
        else:
            for k in range(2):
                pl.when(pl.program_id(0) == k)(
                    functools.partial(store_planes, refs[k - 2], values)
                )

    tile = pl.BlockSpec((CAP, width), lambda j: (0, 0), pipeline_mode=pl.Buffered(1))
    mat = pl.BlockSpec((width, tn), lambda j: (0, skip + j))
    column = (lambda j: (0, 0, j)) if second_half else (lambda j: (0, 0, 0))
    return pl.pallas_call(
        body,
        out_shape=[jax.ShapeDtypeStruct((3, slots, half), BF16)] * outs,
        grid=(half // tn if second_half else 2,),
        in_specs=[tile] * (2 * number) + [mat] * 3 + [free] * len(after),
        out_specs=[pl.BlockSpec((3, slots, tn), column)] * outs,
        compiler_params=params(),
        cost_estimate=pl.CostEstimate(
            flops=3 * outs * slots * width * units,
            bytes_accessed=outs * (3 * width * units + 2 * slots * width + 3 * slots * units),
            transcendentals=slots * units,
        ),
        name="units",
    )(*x_tiles, *w_tiles, *mats, *after)


def row_gradients(parts, gate_matrix, up_matrix):
    splits = [len(part) for part in parts]
    values = flat(parts)
    number = len(values)
    slots = sum(part[0].shape[1] for part in parts)
    tiles = slots // CAP
    width, units = gate_matrix.shape
    tn = tile_of(width, 768, 128)

    def body(*refs):
        value_refs, (gate_ref, up_ref) = refs[:number], refs[number : number + 2]
        outs = refs[number + 2 :]
        grads = dot_nt(planes(value_refs, splits, 1), gate_ref[...])
        grads = grads + dot_nt(planes(value_refs, splits, 2), up_ref[...])
        grads = grads.astype(BF16)
        for r in range(tiles):
            outs[r][...] = grads[r * CAP : (r + 1) * CAP]

    mat = pl.BlockSpec((tn, units), lambda j: (j, 0))
    return pl.pallas_call(
        body,
        out_shape=[jax.ShapeDtypeStruct((CAP, width), BF16)] * tiles,
        grid=(width // tn,),
        in_specs=held(values) + [mat] * 2,
        out_specs=[pl.BlockSpec((CAP, tn), lambda j: (0, j))] * tiles,
        compiler_params=params(),
        cost_estimate=pl.CostEstimate(
            flops=4 * slots * width * units,
            bytes_accessed=2 * (2 * width * units + slots * width + 3 * slots * units),
            transcendentals=0,
        ),
        name="rows",
    )(*values, gate_matrix, up_matrix)


def square_sum(ids, x_tiles, w_tiles, parts, rows, owners):
    number = len(x_tiles)
    width = x_tiles[0].shape[1]
    units = sum(piece.shape[2] for piece in parts[0])
    splits = [len(part) for part in parts]
    values = flat(parts)
    turned = rows % 128 == 0
    tm = rows if turned else tile_of(width, 384, 128)
    slots = number * CAP

    def body(ids_ref, *refs):
        x, w = stacked(refs[:number]), stacked(refs[number : 2 * number])
        value_refs = refs[2 * number : 2 * number + len(values)]
        out_ref, *own_refs, acc = refs[2 * number + len(values) :]

        @pl.when(pl.program_id(0) == 0)
        def _():
            acc[...] = jnp.zeros_like(acc)

        if turned:

            for k, owner in enumerate(owners):

                @pl.when(pl.program_id(0) == owner(ids_ref[0]))
                def _(k=k):
                    own_refs[2 * k][...] = x.T
                    own_refs[2 * k + 1][...] = w.T

        total = acc[...]
        for k, left in enumerate((w, x, x)):
            grads = dot_tn(left, planes(value_refs, splits, k)).astype(BF16).astype(F32)
            total = total + jnp.sum((grads * grads).reshape(tm // 8, 8, units), axis=0)
        acc[...] = total

        @pl.when(pl.program_id(0) == pl.num_programs(0) - 1)
        def _():
            out_ref[...] = jnp.full((8, 128), jnp.sum(acc[...]), F32)

    tile = pl.BlockSpec((CAP, tm), lambda j, ids: (0, j))
    out = pl.pallas_call(
        body,
        out_shape=[jax.ShapeDtypeStruct((8, 128), F32)]
        + [jax.ShapeDtypeStruct((rows, slots), BF16)] * (2 * len(owners) * turned),
        grid_spec=pltpu.PrefetchScalarGridSpec(
            num_scalar_prefetch=1,
            grid=(width // tm,),
            in_specs=[tile] * (2 * number) + held(values),
            out_specs=[pl.BlockSpec((8, 128), lambda j, ids: (0, 0))]
            + [pl.BlockSpec((rows, slots), lambda j, ids: (0, 0))] * (2 * len(owners) * turned),
            scratch_shapes=[pltpu.VMEM((8, units), F32)],
        ),
        compiler_params=params(),
        cost_estimate=pl.CostEstimate(
            flops=6 * slots * width * units,
            bytes_accessed=2 * (2 * slots * width + 3 * slots * units),
            transcendentals=0,
        ),
        name="squares",
    )(ids, *x_tiles, *w_tiles, *values)
    if turned:
        return out

    def rows_of(tiles, index):
        mine = [lax.dynamic_slice_in_dim(tile, index * rows, rows, 1) for tile in tiles]
        return jnp.concatenate(mine, axis=0)

    result = [out[0]]
    for owner in owners:
        index = owner(ids[0])
        result += own_columns(rows_of(x_tiles, index), rows_of(w_tiles, index))
    return result


def own_columns(x_own, w_own):
    slots, rows = x_own.shape

    def body(x_ref, w_ref, xt_ref, wt_ref):
        xt_ref[...] = x_ref[...].T
        wt_ref[...] = w_ref[...].T

    return pl.pallas_call(
        body,
        out_shape=[jax.ShapeDtypeStruct((rows, slots), BF16)] * 2,
        compiler_params=pltpu.CompilerParams(vmem_limit_bytes=VMEM),
        name="own",
    )(x_own, w_own)


def gradient_rows(x_ref, w_ref, refs):
    x, w = x_ref[...], w_ref[...]
    for k, left in enumerate((w, x, x)):
        value = jnp.concatenate([ref[k] for ref in refs], axis=0)
        yield (k + 2) % 3, dot_nn(left, value).astype(BF16)


def rows_cost(halves, slots, rows, units):
    return pl.CostEstimate(
        flops=3 * halves * slots * rows * units,
        bytes_accessed=halves * (2 * slots * rows + 3 * (slots + rows) * units),
        transcendentals=0,
    )


def clipped_rows(ids, scale, x_own, w_own, groups, out, owner, shards, only=None):
    rows, slots = x_own.shape
    half = groups[0][0].shape[2]
    number = len(groups[0])
    halves = len(groups)
    operands = [ids, scale, x_own, w_own, *flat(groups)]
    specs = [pl.BlockSpec(memory_space=pltpu.SMEM)]
    specs += [pl.BlockSpec((rows, slots), lambda j, ids: (0, 0))] * 2 + held(flat(groups))

    def body(ids_ref, scale_ref, x_ref, w_ref, *rest):
        for h in range(halves):
            part = rest[h * number : (h + 1) * number]
            for k, grads in gradient_rows(x_ref, w_ref, part):
                clipped = (grads.astype(F32) * scale_ref[0, 0]).astype(BF16)
                rest[-1][k, :, h * half : (h + 1) * half] = clipped

    if only is None:
        column = lambda j, ids: (0, 0, owner(ids[0]))
    else:
        column = lambda j, ids: (0, 0, owner(ids[0]) * 2 + only)
    aliases = {}
    if out is not None:
        aliases = {len(operands): 0}
        operands.append(out)
        specs.append(free)
    return pl.pallas_call(
        body,
        out_shape=jax.ShapeDtypeStruct((3, rows, 2 * half * shards), BF16),
        grid_spec=pltpu.PrefetchScalarGridSpec(
            num_scalar_prefetch=1,
            grid=(1,),
            in_specs=specs,
            out_specs=pl.BlockSpec((3, rows, halves * half), column),
        ),
        input_output_aliases=aliases,
        compiler_params=params(),
        cost_estimate=rows_cost(halves, slots, rows, 2 * half),
        name="clip",
    )(*operands)


def given_rows(x_other, w_other, group):
    rows, slots = x_other.shape
    half = group[0].shape[2]
    tn = tile_of(half, 256, 128)

    def body(x_ref, w_ref, *rest):
        for k, grads in gradient_rows(x_ref, w_ref, rest[:-1]):
            rest[-1][k] = grads

    block = lambda size: pl.BlockSpec((3, size, tn), lambda j: (0, 0, j))
    return pl.pallas_call(
        body,
        out_shape=jax.ShapeDtypeStruct((3, rows, half), BF16),
        grid=(half // tn,),
        in_specs=[pl.BlockSpec((rows, slots), lambda j: (0, 0))] * 2
        + [block(piece.shape[1]) for piece in group],
        out_specs=block(rows),
        compiler_params=params(),
        cost_estimate=rows_cost(1, slots, rows, 2 * half),
        name="give",
    )(x_other, w_other, *group)


def placed_rows(ids, scale, first, second, out, owners, tokens=None):
    _, rows, half = first.shape
    block = pl.BlockSpec((3, rows, half), lambda j, ids: (0, 0, 0))
    operands = [ids, scale, first, second]
    specs = [pl.BlockSpec(memory_space=pltpu.SMEM), block, block]
    out_shape = [jax.ShapeDtypeStruct(out.shape, BF16)]

    def column(j, ids):
        return (0, 0, jnp.where(j == 0, owners[0](ids[0]) * 2, owners[1](ids[0]) * 2 + 1))

    out_specs = [pl.BlockSpec((3, rows, half), column)]
    others = []
    if tokens is not None:
        mine, others = tokens
        count = mine.shape[2]
        operands += [mine, *others]
        specs.append(pl.BlockSpec((1, rows, count), lambda j, ids: (ids[0] // 2, 0, 0)))
        specs += [pl.BlockSpec((rows, count), lambda j, ids: (0, 0)) for _ in others]
        out_shape.append(jax.ShapeDtypeStruct((rows, count), BF16))
        out_specs.append(pl.BlockSpec((rows, count), lambda j, ids: (0, 0)))
    aliases = {len(operands): 0}
    operands.append(out)
    specs.append(free)

    def body(ids_ref, scale_ref, first_ref, second_ref, *rest):
        out_ref = rest[-len(out_shape)]
        for j, ref in enumerate((first_ref, second_ref)):

            @pl.when(pl.program_id(0) == j)
            def _(ref=ref):
                out_ref[...] = (ref[...].astype(F32) * scale_ref[0, 0]).astype(BF16)

        if tokens is not None:

            @pl.when(pl.program_id(0) == 0)
            def _():
                total = rest[0][0]
                for part in rest[1 : 1 + len(others)]:
                    total = total + part[...].astype(F32)
                rest[-1][...] = total.astype(BF16)

    return pl.pallas_call(
        body,
        out_shape=out_shape,
        grid_spec=pltpu.PrefetchScalarGridSpec(
            num_scalar_prefetch=1, grid=(2,), in_specs=specs, out_specs=out_specs
        ),
        input_output_aliases=aliases,
        compiler_params=params(),
        cost_estimate=pl.CostEstimate(
            flops=6 * rows * half, bytes_accessed=24 * rows * half, transcendentals=0
        ),
        name="place",
    )(*operands)


def token_sums(tiles, picks):
    number = len(tiles)
    width = tiles[0].shape[1]
    count = picks[0].shape[1]
    tn = tile_of(width, 768, 128)

    def body(*refs):
        rows, pick = stacked(refs[:number]), stacked(refs[number : 2 * number])
        refs[2 * number][...] = dot_tn(rows, pick)

    return pl.pallas_call(
        body,
        out_shape=jax.ShapeDtypeStruct((width, count), F32),
        grid=(width // tn,),
        in_specs=[pl.BlockSpec((CAP, tn), lambda j: (0, j))] * number
        + [pl.BlockSpec((CAP, count), lambda j: (0, 0))] * number,
        out_specs=pl.BlockSpec((tn, count), lambda j: (j, 0)),
        compiler_params=params(),
        cost_estimate=pl.CostEstimate(
            flops=2 * number * CAP * width * count,
            bytes_accessed=2 * number * CAP * width + 4 * width * count,
            transcendentals=0,
        ),
        name="combine",
    )(*tiles, *picks)


def per_device(tokens, cotangent, routes, gate_values, gate_weight, up_weight, down_weight):
    experts = lax.axis_size("expert")
    shards = lax.axis_size("dp")
    width = tokens.shape[1]
    gate_matrix, up_matrix, down_matrix = gate_weight[0], up_weight[0], down_weight[0]
    units = gate_matrix.shape[1]
    half = shards // 2
    rows = width // shards
    ids = jnp.stack([lax.axis_index("dp"), lax.axis_index("expert")]).astype(jnp.int32)

    def swap(value, axis, size, bit):
        return lax.ppermute(value, axis, [(i, i ^ bit) for i in range(size)])

    mats = (gate_matrix, up_matrix, down_matrix)
    near = min(2, experts)
    middle = (near + experts) // 2
    groups = [range(r, r + 1) for r in range(near)]
    groups += [g for g in (range(near, middle), range(middle, experts)) if len(g)]
    inputs = (routes.T, gate_values.T, tokens, cotangent)
    value, x_send, w_send, picks = first_units(*inputs, mats, range(near))
    x_tiles, w_tiles = [x_send[0]], [w_send[0]]
    (other,) = expert_units(x_tiles, w_tiles, mats, [value], second_half=True)
    own = [(value, other)]
    if experts > near:
        more = fill_tiles(ids, *inputs, range(near, experts))
        x_send, w_send, picks = [list(p) + list(q) for p, q in zip((x_send, w_send, picks), more)]
    for r in range(1, experts):
        x_tiles.append(swap(x_send[r], "expert", experts, r))
        w_tiles.append(swap(w_send[r], "expert", experts, r))
    for group in groups[1:]:
        part = slice(group[0], group[-1] + 1)
        own.append(tuple(expert_units(x_tiles[part], w_tiles[part], mats, [own[-1][-1]])))

    order = [2 * i for i in range(half)] + [2 * i + 1 for i in reversed(range(half))]
    right = [(order[p], order[(p + 1) % shards]) for p in range(shards)]
    left = [(b, a) for a, b in right]

    def owner_at(step):
        def owner(index):
            place = jnp.where(index % 2 == 0, index // 2, shards - 1 - index // 2)
            source = (place + shards - step) % shards
            return jnp.where(source < half, 2 * source, 2 * (shards - 1 - source) + 1)

        return owner

    def pass_on(value, way):
        return lax.ppermute(value, "dp", right if way == "r" else left)

    def hop(parts, way, halves=(0, 1)):
        return [{h: pass_on(part[h], way) for h in halves} for part in parts]

    def half_of(parts, h):
        return [part[h] for part in parts]

    total, x_own, w_own, x_right, w_right, x_left, w_left = square_sum(
        ids, x_tiles, w_tiles, own, rows, (owner_at(0), owner_at(-1), owner_at(1))
    )

    chunks = {0: own}
    from_left, from_right = own, own
    for step in range(1, half - 1):
        from_left, from_right = hop(from_left, "r"), hop(from_right, "l")
        chunks[step] = from_left
        chunks[shards - step] = from_right
    give = given_rows(x_right, w_right, half_of(from_left, 1))
    right_b = pass_on(give, "r")
    give = given_rows(x_left, w_left, half_of(from_right, 0))
    left_a = pass_on(give, "l")
    from_left = hop(from_left, "r", (0,))
    from_right = hop(from_right, "l", (1,))
    give = given_rows(x_right, w_right, half_of(from_left, 0))
    right_a = pass_on(give, "r")
    give = given_rows(x_left, w_left, half_of(from_right, 1))
    left_b = pass_on(give, "l")

    bit = 1
    while bit < experts:
        total = total + swap(total, "expert", experts, bit)
        bit *= 2
    shares = [total]
    for k in range(1, shards):
        shares.append(swap(total, "dp", shards, k))
    total = functools.reduce(lambda a, b: a + b, shares)
    clip_limit = CLIP_RMS * math.sqrt(3.0 * experts * width * units * shards)
    scale = clip_limit / jnp.maximum(jnp.sqrt(total[0:1, 0:1]), clip_limit)

    sent = []
    for part in [own[:near]] + [[part] for part in own[near:]]:
        sent += row_gradients(part, gate_matrix, up_matrix)
    back = sent[:1]
    for r in range(1, experts):
        back.append(swap(sent[r], "expert", experts, r))
    outer, inner = ids[0] // 2, ids[0] % 2
    partial = token_sums(back, picks).reshape(half, 2, rows, tokens.shape[0])
    send = lax.dynamic_index_in_dim(partial, 1 - inner, 1, keepdims=False).astype(BF16)
    keep = lax.dynamic_index_in_dim(partial, inner, 1, keepdims=False)
    other = swap(send, "dp", shards, 1)
    sums = keep + other.astype(F32)
    parts = []
    for turn in range(1, half):
        part = lax.dynamic_index_in_dim(sums, (outer + turn) % half, 0, keepdims=False).astype(BF16)
        route = [(2 * i + j, 2 * ((i + turn) % half) + j) for i in range(half) for j in range(2)]
        parts.append(lax.ppermute(part, "dp", route))
    common = (ids, scale, x_own, w_own)
    out = None
    for step in clip_order(shards):
        groups = [half_of(chunks[step], h) for h in range(2)]
        out = clipped_rows(*common, groups, out, owner_at(step), shards)
    for h, step, parts_at in ((0, half - 1, from_left), (1, half + 1, from_right)):
        group = [half_of(parts_at, h)]
        out = clipped_rows(*common, group, out, owner_at(step), shards, only=h)
    owners = (owner_at(half + 1), owner_at(half - 1))
    (out,) = placed_rows(ids, scale, left_a, right_b, out, owners)
    owners = (owner_at(half), owner_at(half))
    out, d_tokens = placed_rows(ids, scale, right_a, left_b, out, owners, (sums, parts))
    return (out[None], d_tokens)


def clip_order(shards):
    return [0] + [s for step in range(1, shards // 2 - 1) for s in (step, shards - step)]


def solution(mesh):
    return jax.shard_map(
        per_device,
        mesh=mesh,
        in_specs=(
            P("expert", None),
            P("expert", None),
            P("expert", None),
            P("expert", None),
            P("expert", None, "dp"),
            P("expert", None, "dp"),
            P("expert", None, "dp"),
        ),
        out_specs=(P("expert", None, "dp", None), P("dp", "expert")),
        check_vma=False,
    )
```

profile of v0, /device:TPU:0, one launch (start us, length us, event | category | flops | bytes accessed | tf_op | source)
XLA Modules:
  0.0 401.1 jit_solution(6210142137076874540)
XLA Ops:
  0.6 7.9 %first.1 = (bf16[3,128,512]{2,1,0:T(8,128)(2,1)}, bf16[128,3072]{1,0:T(8,128)(2,1)}, bf16[128,3072]{1,0:T(8,128)(2,1)}, bf16[128,3072]{1,0:T(8,128)(2,1)}, bf16[...) custom-call(s32[2,256]{1,0:T(2,128)} %bitcast.47, bf16[2,256]{1,0:T(2,128)(2,1)} %bitcast.49, ...), custom_call_target="tpu_custom_call" | custom-call | flops 1207959552 | bytes 15728640 | tf_op jit(solution)/shard_map/first/pallas_call | solution.py:183
  9.8 4.6 %fill.1 = (bf16[128,3072]{1,0:T(8,128)(2,1)}, bf16[128,3072]{1,0:T(8,128)(2,1)}, bf16[128,3072]{1,0:T(8,128)(2,1)}, bf16[128,3072]{1,0:T(8,128)(2,1)}, bf16[128,...) custom-call(s32[2]{0:T(128)} %pad_add_fusion.ids_ref, s32[2,256]{1,0:T(2,128)} %bitcast.48, bf16[2,256]{1,0:T(2,128)(2,1)} %bitcast.50, ...), custom_call_target="tpu_custom_call" | custom-call | flops 805306368 | bytes 6291456 | tf_op jit(solution)/shard_map/fill/pallas_call | solution.py:122
  17.3 5.7 %units.4.refs_5_.refs_9_.refs_1_.rest_4_ = bf16[3,128,512]{2,1,0:T(8,128)(2,1)} custom-call(bf16[128,3072]{1,0:T(8,128)(2,1)} %get-tuple-element.32.refs_0_, bf16[128,3072]{1,0:T(8,128)(2,1)} %get-tuple-element.36.refs_1_.refs_4_, bf16[3072,1024]{1,0:T(8,128)(2,1)} %bitcast.25, bf16[3072,1024]{1,0:T(8,128)(2,1)} %bitcast.33, bf16[3072,1024]{1,0:T(8,128)(2,1)} %bitcast.41, ...), custom_call_target="tpu_custom_call" | custom-call | flops 1207959552 | bytes 10616832 | tf_op jit(solution)/shard_map/units/pallas_call | solution.py:232
  25.1 9.1 %collective-permute-done.57.rest_4_ = bf16[3,128,512]{2,1,0:T(8,128)(2,1)} collective-permute-done((bf16[3,128,512]{2,1,0:T(8,128)(2,1)}, bf16[3,128,512]{2,1,0:T(8,128)(2,1)}, u32[]{:S(2)}, u32[]{:S(2)}) %collective-permute-start.57) | collective-permute-done | bytes 393248 | tf_op jit(solution)/shard_map/ppermute | solution.py:579
  38.0 14.8 %collective-permute-done.4.refs_1_.refs_6_ = bf16[128,3072]{1,0:T(8,128)(2,1)} collective-permute-done((bf16[128,3072]{1,0:T(8,128)(2,1)}, bf16[128,3072]{1,0:T(8,128)(2,1)}, u32[]{:S(2)}, u32[]{:S(2)}) %collective-permute-start.4) | collective-permute-done | bytes 786464 | tf_op jit(solution)/shard_map/ppermute | solution.py:544
  54.8 9.3 %units.5 = (bf16[3,128,512]{2,1,0:T(8,128)(2,1)}, bf16[3,128,512]{2,1,0:T(8,128)(2,1)}) custom-call(bf16[128,3072]{1,0:T(8,128)(2,1)} %collective-permute-done.refs_0_.refs_1_, bf16[128,3072]{1,0:T(8,128)(2,1)} %collective-permute-done.3.refs_1_.refs_5_, bf16[3072,1024]{1,0:T(8,128)(2,1)} %bitcast.26, bf16[3072,1024]{1,0:T(8,128)(2,1)} %bitcast.34, ...), custom_call_target="tpu_custom_call" | custom-call | flops 2415919104 | bytes 21233664 | tf_op jit(solution)/shard_map/units/pallas_call | solution.py:232
  64.1 9.4 %units.6 = (bf16[3,128,512]{2,1,0:T(8,128)(2,1)}, bf16[3,128,512]{2,1,0:T(8,128)(2,1)}) custom-call(bf16[128,3072]{1,0:T(8,128)(2,1)} %collective-permute-done.1.refs_0_.refs_2_, bf16[128,3072]{1,0:T(8,128)(2,1)} %collective-permute-done.4.refs_1_.refs_6_, bf16[3072,1024]{1,0:T(8,128)(2,1)} %bitcast.27, bf16[3072,1024]{1,0:T(8,128)(2,1)} %bitcast.35, ...), custom_call_target="tpu_custom_call" | custom-call | flops 2415919104 | bytes 21233664 | tf_op jit(solution)/shard_map/units/pallas_call | solution.py:232
  77.5 7.7 %collective-permute-done.5.refs_1_.refs_7_ = bf16[128,3072]{1,0:T(8,128)(2,1)} collective-permute-done((bf16[128,3072]{1,0:T(8,128)(2,1)}, bf16[128,3072]{1,0:T(8,128)(2,1)}, u32[]{:S(2)}, u32[]{:S(2)}) %collective-permute-start.5) | collective-permute-done | bytes 786464 | tf_op jit(solution)/shard_map/ppermute | solution.py:544
  85.3 9.3 %units.7 = (bf16[3,128,512]{2,1,0:T(8,128)(2,1)}, bf16[3,128,512]{2,1,0:T(8,128)(2,1)}) custom-call(bf16[128,3072]{1,0:T(8,128)(2,1)} %collective-permute-done.2.refs_0_.refs_3_, bf16[128,3072]{1,0:T(8,128)(2,1)} %collective-permute-done.5.refs_1_.refs_7_, bf16[3072,1024]{1,0:T(8,128)(2,1)} %bitcast.28, bf16[3072,1024]{1,0:T(8,128)(2,1)} %bitcast.36, ...), custom_call_target="tpu_custom_call" | custom-call | flops 2415919104 | bytes 21233664 | tf_op jit(solution)/shard_map/units/pallas_call | solution.py:232
  94.6 18.2 %squares.1 = (f32[8,128]{1,0:T(8,128)}, bf16[384,512]{1,0:T(8,128)(2,1)}, bf16[384,512]{1,0:T(8,128)(2,1)}, bf16[384,512]{1,0:T(8,128)(2,1)}, bf16[384,512]{1,0:...) custom-call(s32[2]{0:T(128)} %pad_add_fusion.ids_ref, bf16[128,3072]{1,0:T(8,128)(2,1)} %get-tuple-element.32.refs_0_, ...), custom_call_target="tpu_custom_call" | custom-call | flops 9663676416 | bytes 9437184 | tf_op jit(solution)/shard_map/squares/pallas_call | solution.py:322
  125.3 19.1 %collective-permute-done.10 = f32[8,128]{1,0:T(8,128)S(1)} collective-permute-done((f32[8,128]{1,0:T(8,128)S(1)}, f32[8,128]{1,0:T(8,128)S(1)}, u32[]{:S(2)}, u32[]{:S(2)}) %collective-permute-start.10) | collective-permute-done | bytes 4128 | tf_op jit(solution)/shard_map/ppermute | solution.py:544
  160.4 5.3 %collective-permute-done.21.rest_2_ = bf16[3,128,512]{2,1,0:T(8,128)(2,1)} collective-permute-done((bf16[3,128,512]{2,1,0:T(8,128)(2,1)}, bf16[3,128,512]{2,1,0:T(8,128)(2,1)}, u32[]{:S(2)}, u32[]{:S(2)}) %collective-permute-start.21) | collective-permute-done | bytes 393248 | tf_op jit(solution)/shard_map/ppermute | solution.py:579
  166.1 8.0 %collective-permute-done.59.rest_5_ = bf16[3,128,512]{2,1,0:T(8,128)(2,1)} collective-permute-done((bf16[3,128,512]{2,1,0:T(8,128)(2,1)}, bf16[3,128,512]{2,1,0:T(8,128)(2,1)}, u32[]{:S(2)}, u32[]{:S(2)}) %collective-permute-start.59) | collective-permute-done | bytes 393248 | tf_op jit(solution)/shard_map/ppermute | solution.py:579
  174.6 4.8 %collective-permute-done.18.rest_1_ = bf16[3,128,512]{2,1,0:T(8,128)(2,1)} collective-permute-done((bf16[3,128,512]{2,1,0:T(8,128)(2,1)}, bf16[3,128,512]{2,1,0:T(8,128)(2,1)}, u32[]{:S(2)}, u32[]{:S(2)}) %collective-permute-start.18) | collective-permute-done | bytes 393248 | tf_op jit(solution)/shard_map/ppermute | solution.py:579
  181.8 4.7 %collective-permute-done.34.rest_6_ = bf16[3,128,512]{2,1,0:T(8,128)(2,1)S(1)} collective-permute-done((bf16[3,128,512]{2,1,0:T(8,128)(2,1)}, bf16[3,128,512]{2,1,0:T(8,128)(2,1)S(1)}, u32[]{:S(2)}, u32[]{:S(2)}) %collective-permute-start.34) | collective-permute-done | bytes 393248 | tf_op jit(solution)/shard_map/ppermute | solution.py:579
  187.3 7.7 %collective-permute-done.52.rest_2_ = bf16[3,128,512]{2,1,0:T(8,128)(2,1)S(1)} collective-permute-done((bf16[3,128,512]{2,1,0:T(8,128)(2,1)}, bf16[3,128,512]{2,1,0:T(8,128)(2,1)S(1)}, u32[]{:S(2)}, u32[]{:S(2)}) %collective-permute-start.52) | collective-permute-done | bytes 393248 | tf_op jit(solution)/shard_map/ppermute | solution.py:579
  196.9 6.5 %collective-permute-done.31.rest_5_ = bf16[3,128,512]{2,1,0:T(8,128)(2,1)S(1)} collective-permute-done((bf16[3,128,512]{2,1,0:T(8,128)(2,1)}, bf16[3,128,512]{2,1,0:T(8,128)(2,1)S(1)}, u32[]{:S(2)}, u32[]{:S(2)}) %collective-permute-start.31) | collective-permute-done | bytes 393248 | tf_op jit(solution)/shard_map/ppermute | solution.py:579
  205.3 6.0 %collective-permute-done.50.rest_1_ = bf16[3,128,512]{2,1,0:T(8,128)(2,1)S(1)} collective-permute-done((bf16[3,128,512]{2,1,0:T(8,128)(2,1)}, bf16[3,128,512]{2,1,0:T(8,128)(2,1)S(1)}, u32[]{:S(2)}, u32[]{:S(2)}) %collective-permute-start.50) | collective-permute-done | bytes 393248 | tf_op jit(solution)/shard_map/ppermute | solution.py:579
  220.3 8.4 %rows.5 = bf16[128,3072]{1,0:T(8,128)(2,1)} custom-call(bf16[3,128,512]{2,1,0:T(8,128)(2,1)} %get-tuple-element.45.refs_14_.refs_0_.rest_3_, bf16[3,128,512]{2,1,0:T(8,128)(2,1)} %get-tuple-element.46.refs_15_.refs_1_.rest_7_, bf16[3072,1024]{1,0:T(8,128)(2,1)} %bitcast.29, bf16[3072,1024]{1,0:T(8,128)(2,1)} %bitcast.37), custom_call_target="tpu_custom_call" | custom-call | flops 1610612736 | bytes 14155776 | tf_op jit(solution)/shard_map/rows/pallas_call | solution.py:267
  233.1 8.4 %rows.3 = (bf16[128,3072]{1,0:T(8,128)(2,1)}, bf16[128,3072]{1,0:T(8,128)(2,1)}) custom-call(bf16[3,128,512]{2,1,0:T(8,128)(2,1)} %get-tuple-element.40.refs_5_.refs_8_.refs_0_.rest_0_, bf16[3,128,512]{2,1,0:T(8,128)(2,1)} %units.4.refs_5_.refs_9_.refs_1_.rest_4_, bf16[3,128,512]{2,1,0:T(8,128)(2,1)} %get-tuple-element.41.refs_10_.refs_2_.rest_1_, ...), custom_call_target="tpu_custom_call" | custom-call | flops 3221225472 | bytes 15728640 | tf_op jit(solution)/shard_map/rows/pallas_call | solution.py:267
  245.1 8.4 %rows.4 = bf16[128,3072]{1,0:T(8,128)(2,1)} custom-call(bf16[3,128,512]{2,1,0:T(8,128)(2,1)} %get-tuple-element.43.refs_12_.refs_0_.rest_2_, bf16[3,128,512]{2,1,0:T(8,128)(2,1)} %get-tuple-element.44.refs_5_.refs_13_.refs_1_.rest_6_, bf16[3072,1024]{1,0:T(8,128)(2,1)} %bitcast.31, bf16[3072,1024]{1,0:T(8,128)(2,1)} %bitcast.39), custom_call_target="tpu_custom_call" | custom-call | flops 1610612736 | bytes 14155776 | tf_op jit(solution)/shard_map/rows/pallas_call | solution.py:267
  257.2 9.7 %collective-permute-done.32.rest_5_ = bf16[3,128,512]{2,1,0:T(8,128)(2,1)} collective-permute-done((bf16[3,128,512]{2,1,0:T(8,128)(2,1)}, bf16[3,128,512]{2,1,0:T(8,128)(2,1)}, u32[]{:S(2)}, u32[]{:S(2)}) %collective-permute-start.32) | collective-permute-done | bytes 393248 | tf_op jit(solution)/shard_map/ppermute | solution.py:579
  268.2 6.2 %collective-permute-done.51.rest_1_ = bf16[3,128,512]{2,1,0:T(8,128)(2,1)} collective-permute-done((bf16[3,128,512]{2,1,0:T(8,128)(2,1)}, bf16[3,128,512]{2,1,0:T(8,128)(2,1)}, u32[]{:S(2)}, u32[]{:S(2)}) %collective-permute-start.51) | collective-permute-done | bytes 393248 | tf_op jit(solution)/shard_map/ppermute | solution.py:579
  291.3 5.3 %combine.1 = f32[3072,256]{1,0:T(8,128)} custom-call(bf16[128,3072]{1,0:T(8,128)(2,1)} %get-tuple-element.52.refs_0_, bf16[128,3072]{1,0:T(8,128)(2,1)} %collective-permute-done.41.refs_1_, bf16[128,3072]{1,0:T(8,128)(2,1)} %collective-permute-done.42.refs_2_, bf16[128,3072]{1,0:T(8,128)(2,1)} %collective-permute-done.43.refs_3_, ...), custom_call_target="tpu_custom_call" | custom-call | flops 805306368 | bytes 6291456 | tf_op jit(solution)/shard_map/combine/pallas_call | solution.py:516
  314.0 29.6 %collective-permute-done.8 = f32[8,128]{1,0:T(8,128)} collective-permute-done((f32[8,128]{1,0:T(8,128)}, f32[8,128]{1,0:T(8,128)}, u32[]{:S(2)}, u32[]{:S(2)}) %collective-permute-start.8) | collective-permute-done | bytes 4128 | tf_op jit(solution)/shard_map/ppermute | solution.py:544
  347.6 5.5 %clip.7.rest_8_ = bf16[3,384,8192]{2,1,0:T(8,128)(2,1)} custom-call(s32[2]{0:T(128)} %pad_add_fusion.ids_ref, f32[1,1]{1,0:T(1,128)S(6)} %div.11.scale_ref, bf16[384,512]{1,0:T(8,128)(2,1)} %get-tuple-element.58.x_ref, bf16[384,512]{1,0:T(8,128)(2,1)} %get-tuple-element.59.w_ref, bf16[3,128,512]{2,1,0:T(8,128)(2,1)} %get-tuple-element.40.refs_5_.refs_8_.refs_0_.rest_0_, ...), custom_call_target="tpu_custom_call" | custom-call | flops 1207959552 | bytes 6291456 | tf_op jit(solution)/shard_map/clip/pallas_call | solution.py:411
  353.1 5.5 %clip.8.rest_8_ = bf16[3,384,8192]{2,1,0:T(8,128)(2,1)} custom-call(s32[2]{0:T(128)} %pad_add_fusion.ids_ref, f32[1,1]{1,0:T(1,128)S(6)} %div.11.scale_ref, bf16[384,512]{1,0:T(8,128)(2,1)} %get-tuple-element.58.x_ref, bf16[384,512]{1,0:T(8,128)(2,1)} %get-tuple-element.59.w_ref, ...), custom_call_target="tpu_custom_call", output_to_operand_aliasing={{}: (12, {})} | custom-call | flops 1207959552 | bytes 6291456 | tf_op jit(solution)/shard_map/clip/pallas_call | solution.py:411
  358.7 5.5 %clip.9.rest_8_ = bf16[3,384,8192]{2,1,0:T(8,128)(2,1)} custom-call(s32[2]{0:T(128)} %pad_add_fusion.ids_ref, f32[1,1]{1,0:T(1,128)S(6)} %div.11.scale_ref, bf16[384,512]{1,0:T(8,128)(2,1)} %get-tuple-element.58.x_ref, bf16[384,512]{1,0:T(8,128)(2,1)} %get-tuple-element.59.w_ref, ...), custom_call_target="tpu_custom_call", output_to_operand_aliasing={{}: (12, {})} | custom-call | flops 1207959552 | bytes 6291456 | tf_op jit(solution)/shard_map/clip/pallas_call | solution.py:411
  364.2 5.5 %clip.10.rest_8_ = bf16[3,384,8192]{2,1,0:T(8,128)(2,1)} custom-call(s32[2]{0:T(128)} %pad_add_fusion.ids_ref, f32[1,1]{1,0:T(1,128)S(6)} %div.11.scale_ref, bf16[384,512]{1,0:T(8,128)(2,1)} %get-tuple-element.58.x_ref, bf16[384,512]{1,0:T(8,128)(2,1)} %get-tuple-element.59.w_ref, ...), custom_call_target="tpu_custom_call", output_to_operand_aliasing={{}: (12, {})} | custom-call | flops 1207959552 | bytes 6291456 | tf_op jit(solution)/shard_map/clip/pallas_call | solution.py:411
  373.5 4.7 %collective-permute-start.46 = (bf16[384,256]{1,0:T(8,128)(2,1)}, bf16[384,256]{1,0:T(8,128)(2,1)}, u32[]{:S(2)}, u32[]{:S(2)}) collective-permute-start(bf16[384,256]{1,0:T(8,128)(2,1)} %get-tuple-element.63), channel_id=1, source_target_pairs={{0,16},{4,20},{8,24},{12,28},{16,0},{20,4},{24,8},{28,12},{1,17},{... | collective-permute-start | bytes 589832 | tf_op jit(solution)/shard_map/ppermute | solution.py:635
  379.1 5.5 %clip.11.rest_4_ = bf16[3,384,8192]{2,1,0:T(8,128)(2,1)} custom-call(s32[2]{0:T(128)} %pad_add_fusion.ids_ref, f32[1,1]{1,0:T(1,128)S(6)} %div.11.scale_ref, bf16[384,512]{1,0:T(8,128)(2,1)} %get-tuple-element.58.x_ref, bf16[384,512]{1,0:T(8,128)(2,1)} %get-tuple-element.59.w_ref, ...), custom_call_target="tpu_custom_call", output_to_operand_aliasing={{}: (12, {})} | custom-call | flops 1207959552 | bytes 6291456 | tf_op jit(solution)/shard_map/clip/pallas_call | solution.py:411
  396.7 4.4 %place.3 = (bf16[3,384,8192]{2,1,0:T(8,128)(2,1)}, bf16[384,256]{1,0:T(8,128)(2,1)}) custom-call(s32[2]{0:T(128)} %pad_add_fusion.ids_ref, f32[1,1]{1,0:T(1,128)S(6)} %div.11.scale_ref, bf16[3,384,512]{2,1,0:T(8,128)(2,1)} %collective-permute-done.27.first_ref, ...), custom_call_target="tpu_custom_call", output_to_operand_aliasing={{0}: (8, {})} | custom-call | flops 1179648 | bytes 4718592 | tf_op jit(solution)/shard_map/place/pallas_call | solution.py:491
  (162 shorter events, 128.9 us)
Async XLA Ops:
  8.5 25.7 %collective-permute-start = (bf16[128,3072]{1,0:T(8,128)(2,1)}, bf16[128,3072]{1,0:T(8,128)(2,1)}, u32[]{:S(2)}, u32[]{:S(2)}) collective-permute-start(bf16[128,3072]{1,0:T(8,128)(2,1)} %get-tuple-element.33), channel_id=1, source_target_pairs={{0,1},{1,0},{2,3},{3,2},{4,5},{5,4},{6,7},{7,6},{8,9},{9,8},{10,11... | collective-permute-start | bytes 2359304 | tf_op jit(solution)/shard_map/ppermute | solution.py:544
  9.0 26.9 %collective-permute-start.3 = (bf16[128,3072]{1,0:T(8,128)(2,1)}, bf16[128,3072]{1,0:T(8,128)(2,1)}, u32[]{:S(2)}, u32[]{:S(2)}) collective-permute-start(bf16[128,3072]{1,0:T(8,128)(2,1)} %get-tuple-element.37), channel_id=1, source_target_pairs={{0,1},{1,0},{2,3},{3,2},{4,5},{5,4},{6,7},{7,6},{8,9},{9,8},{10,11... | collective-permute-start | bytes 2359304 | tf_op jit(solution)/shard_map/ppermute | solution.py:544
  17.2 35.6 %collective-permute-start.4 = (bf16[128,3072]{1,0:T(8,128)(2,1)}, bf16[128,3072]{1,0:T(8,128)(2,1)}, u32[]{:S(2)}, u32[]{:S(2)}) collective-permute-start(bf16[128,3072]{1,0:T(8,128)(2,1)} %get-tuple-element.38), channel_id=1, source_target_pairs={{0,2},{1,3},{2,0},{3,1},{4,6},{5,7},{6,4},{7,5},{8,10},{9,11},{10,... | collective-permute-start | bytes 2359304 | tf_op jit(solution)/shard_map/ppermute | solution.py:544
  34.2 41.4 %collective-permute-start.2 = (bf16[128,3072]{1,0:T(8,128)(2,1)}, bf16[128,3072]{1,0:T(8,128)(2,1)}, u32[]{:S(2)}, u32[]{:S(2)}) collective-permute-start(bf16[128,3072]{1,0:T(8,128)(2,1)} %get-tuple-element.35), channel_id=1, source_target_pairs={{0,3},{1,2},{2,1},{3,0},{4,7},{5,6},{6,5},{7,4},{8,11},{9,10},{10,... | collective-permute-start | bytes 2359304 | tf_op jit(solution)/shard_map/ppermute | solution.py:544
  34.2 51.1 %collective-permute-start.5 = (bf16[128,3072]{1,0:T(8,128)(2,1)}, bf16[128,3072]{1,0:T(8,128)(2,1)}, u32[]{:S(2)}, u32[]{:S(2)}) collective-permute-start(bf16[128,3072]{1,0:T(8,128)(2,1)} %get-tuple-element.39), channel_id=1, source_target_pairs={{0,3},{1,2},{2,1},{3,0},{4,7},{5,6},{6,5},{7,4},{8,11},{9,10},{10,... | collective-permute-start | bytes 2359304 | tf_op jit(solution)/shard_map/ppermute | solution.py:544
  35.9 37.5 %collective-permute-start.15 = (bf16[3,128,512]{2,1,0:T(8,128)(2,1)}, bf16[3,128,512]{2,1,0:T(8,128)(2,1)}, u32[]{:S(2)}, u32[]{:S(2)}) collective-permute-start(bf16[3,128,512]{2,1,0:T(8,128)(2,1)} %get-tuple-element.40.refs_5_.refs_8_.refs_0_.rest_0_), channel_id=1, source_target_pairs={{0,8},{8,16},{16,24},{24,28},{28,20},{20,12},{12,4},{4,0},{1,9},{9... | collective-permute-start | bytes 1179656 | tf_op jit(solution)/shard_map/ppermute | solution.py:579
  37.7 35.8 %collective-permute-start.28 = (bf16[3,128,512]{2,1,0:T(8,128)(2,1)}, bf16[3,128,512]{2,1,0:T(8,128)(2,1)}, u32[]{:S(2)}, u32[]{:S(2)}) collective-permute-start(bf16[3,128,512]{2,1,0:T(8,128)(2,1)} %units.4.refs_5_.refs_9_.refs_1_.rest_4_), channel_id=1, source_target_pairs={{8,0},{16,8},{24,16},{28,24},{20,28},{12,20},{4,12},{0,4},{9,1},{1... | collective-permute-start | bytes 1179656 | tf_op jit(solution)/shard_map/ppermute | solution.py:579
  73.5 43.6 %collective-permute-start.58 = (bf16[3,128,512]{2,1,0:T(8,128)(2,1)}, bf16[3,128,512]{2,1,0:T(8,128)(2,1)}, u32[]{:S(2)}, u32[]{:S(2)}) collective-permute-start(bf16[3,128,512]{2,1,0:T(8,128)(2,1)} %collective-permute-done.57.rest_4_), channel_id=1, source_target_pairs={{0,8},{8,16},{16,24},{24,28},{28,20},{20,12},{12,4},{4,0},{1,9},{9... | collective-permute-start | bytes 1179656 | tf_op jit(solution)/shard_map/ppermute | solution.py:579
  73.6 45.1 %collective-permute-start.16 = (bf16[3,128,512]{2,1,0:T(8,128)(2,1)}, bf16[3,128,512]{2,1,0:T(8,128)(2,1)}, u32[]{:S(2)}, u32[]{:S(2)}) collective-permute-start(bf16[3,128,512]{2,1,0:T(8,128)(2,1)} %collective-permute-done.15.rest_0_), channel_id=1, source_target_pairs={{0,8},{8,16},{16,24},{24,28},{28,20},{20,12},{12,4},{4,0},{1,9},{9... | collective-permute-start | bytes 1179656 | tf_op jit(solution)/shard_map/ppermute | solution.py:579
  75.6 46.7 %collective-permute-start.29 = (bf16[3,128,512]{2,1,0:T(8,128)(2,1)}, bf16[3,128,512]{2,1,0:T(8,128)(2,1)}, u32[]{:S(2)}, u32[]{:S(2)}) collective-permute-start(bf16[3,128,512]{2,1,0:T(8,128)(2,1)} %collective-permute-done.28.rest_4_), channel_id=1, source_target_pairs={{8,0},{16,8},{24,16},{28,24},{20,28},{12,20},{4,12},{0,4},{9,1},{1... | collective-permute-start | bytes 1179656 | tf_op jit(solution)/shard_map/ppermute | solution.py:579
  75.6 46.9 %collective-permute-start.49 = (bf16[3,128,512]{2,1,0:T(8,128)(2,1)}, bf16[3,128,512]{2,1,0:T(8,128)(2,1)}, u32[]{:S(2)}, u32[]{:S(2)}) collective-permute-start(bf16[3,128,512]{2,1,0:T(8,128)(2,1)} %collective-permute-done.48.rest_0_), channel_id=1, source_target_pairs={{8,0},{16,8},{24,16},{28,24},{20,28},{12,20},{4,12},{0,4},{9,1},{1... | collective-permute-start | bytes 1179656 | tf_op jit(solution)/shard_map/ppermute | solution.py:579
  114.6 41.5 %collective-permute-start.24 = (bf16[3,128,512]{2,1,0:T(8,128)(2,1)}, bf16[3,128,512]{2,1,0:T(8,128)(2,1)S(1)}, u32[]{:S(2)}, u32[]{:S(2)}) collective-permute-start(bf16[3,128,512]{2,1,0:T(8,128)(2,1)} %get-tuple-element.45.refs_14_.refs_0_.rest_3_), channel_id=1, source_target_pairs={{0,8},{8,16},{16,24},{24,28},{28,20},{20,12},{12,4},{4,0},{1,9},{9... | collective-permute-start | bytes 1179656 | tf_op jit(solution)/shard_map/ppermute | solution.py:579
  118.6 38.8 %collective-permute-start.63 = (bf16[3,128,512]{2,1,0:T(8,128)(2,1)}, bf16[3,128,512]{2,1,0:T(8,128)(2,1)S(1)}, u32[]{:S(2)}, u32[]{:S(2)}) collective-permute-start(bf16[3,128,512]{2,1,0:T(8,128)(2,1)} %get-tuple-element.46.refs_15_.refs_1_.rest_7_), channel_id=1, source_target_pairs={{0,8},{8,16},{16,24},{24,28},{28,20},{20,12},{12,4},{4,0},{1,9},{9... | collective-permute-start | bytes 1179656 | tf_op jit(solution)/shard_map/ppermute | solution.py:579
  120.7 37.5 %collective-permute-start.61 = (bf16[3,128,512]{2,1,0:T(8,128)(2,1)}, bf16[3,128,512]{2,1,0:T(8,128)(2,1)}, u32[]{:S(2)}, u32[]{:S(2)}) collective-permute-start(bf16[3,128,512]{2,1,0:T(8,128)(2,1)} %get-tuple-element.44.refs_5_.refs_13_.refs_1_.rest_6_), channel_id=1, source_target_pairs={{0,8},{8,16},{16,24},{24,28},{28,20},{20,12},{12,4},{4,0},{1,9},{9... | collective-permute-start | bytes 1179656 | tf_op jit(solution)/shard_map/ppermute | solution.py:579
  179.8 31.5 %collective-permute-start.50 = (bf16[3,128,512]{2,1,0:T(8,128)(2,1)}, bf16[3,128,512]{2,1,0:T(8,128)(2,1)S(1)}, u32[]{:S(2)}, u32[]{:S(2)}) collective-permute-start(bf16[3,128,512]{2,1,0:T(8,128)(2,1)} %get-tuple-element.41.refs_10_.refs_2_.rest_1_), channel_id=1, source_target_pairs={{8,0},{16,8},{24,16},{28,24},{20,28},{12,20},{4,12},{0,4},{9,1},{1... | collective-permute-start | bytes 1179656 | tf_op jit(solution)/shard_map/ppermute | solution.py:579
  180.4 33.2 %collective-permute-start.17 = (bf16[3,128,512]{2,1,0:T(8,128)(2,1)}, bf16[3,128,512]{2,1,0:T(8,128)(2,1)}, u32[]{:S(2)}, u32[]{:S(2)}) collective-permute-start(bf16[3,128,512]{2,1,0:T(8,128)(2,1)} %collective-permute-done.16.rest_0_), channel_id=1, source_target_pairs={{0,8},{8,16},{16,24},{24,28},{28,20},{20,12},{12,4},{4,0},{1,9},{9... | collective-permute-start | bytes 1179656 | tf_op jit(solution)/shard_map/ppermute | solution.py:579
  186.5 29.1 %collective-permute-start.30 = (bf16[3,128,512]{2,1,0:T(8,128)(2,1)}, bf16[3,128,512]{2,1,0:T(8,128)(2,1)}, u32[]{:S(2)}, u32[]{:S(2)}) collective-permute-start(bf16[3,128,512]{2,1,0:T(8,128)(2,1)} %collective-permute-done.29.rest_4_), channel_id=1, source_target_pairs={{8,0},{16,8},{24,16},{28,24},{20,28},{12,20},{4,12},{0,4},{9,1},{1... | collective-permute-start | bytes 1179656 | tf_op jit(solution)/shard_map/ppermute | solution.py:579
  215.6 25.9 %collective-permute-start.60 = (bf16[3,128,512]{2,1,0:T(8,128)(2,1)}, bf16[3,128,512]{2,1,0:T(8,128)(2,1)}, u32[]{:S(2)}, u32[]{:S(2)}) collective-permute-start(bf16[3,128,512]{2,1,0:T(8,128)(2,1)} %collective-permute-done.59.rest_5_), channel_id=1, source_target_pairs={{0,8},{8,16},{16,24},{24,28},{28,20},{20,12},{12,4},{4,0},{1,9},{9... | collective-permute-start | bytes 1179656 | tf_op jit(solution)/shard_map/ppermute | solution.py:579
  217.9 25.6 %collective-permute-start.19 = (bf16[3,128,512]{2,1,0:T(8,128)(2,1)}, bf16[3,128,512]{2,1,0:T(8,128)(2,1)}, u32[]{:S(2)}, u32[]{:S(2)}) collective-permute-start(bf16[3,128,512]{2,1,0:T(8,128)(2,1)} %collective-permute-done.18.rest_1_), channel_id=1, source_target_pairs={{0,8},{8,16},{16,24},{24,28},{28,20},{20,12},{12,4},{4,0},{1,9},{9... | collective-permute-start | bytes 1179656 | tf_op jit(solution)/shard_map/ppermute | solution.py:579
  228.7 24.8 %collective-permute-start.55 = (bf16[3,128,512]{2,1,0:T(8,128)(2,1)}, bf16[3,128,512]{2,1,0:T(8,128)(2,1)}, u32[]{:S(2)}, u32[]{:S(2)}) collective-permute-start(bf16[3,128,512]{2,1,0:T(8,128)(2,1)} %copy-done.3), channel_id=1, source_target_pairs={{8,0},{16,8},{24,16},{28,24},{20,28},{12,20},{4,12},{0,4},{9,1},{1... | collective-permute-start | bytes 1179656 | tf_op jit(solution)/shard_map/ppermute | solution.py:579
  241.5 34.3 %collective-permute-start.41 = (bf16[128,3072]{1,0:T(8,128)(2,1)}, bf16[128,3072]{1,0:T(8,128)(2,1)}, u32[]{:S(2)}, u32[]{:S(2)}) collective-permute-start(bf16[128,3072]{1,0:T(8,128)(2,1)} %get-tuple-element.53), channel_id=1, source_target_pairs={{0,1},{1,0},{2,3},{3,2},{4,5},{5,4},{6,7},{7,6},{8,9},{9,8},{10,11... | collective-permute-start | bytes 2359304 | tf_op jit(solution)/shard_map/ppermute | solution.py:544
  243.5 33.2 %collective-permute-start.43 = (bf16[128,3072]{1,0:T(8,128)(2,1)}, bf16[128,3072]{1,0:T(8,128)(2,1)}, u32[]{:S(2)}, u32[]{:S(2)}) collective-permute-start(bf16[128,3072]{1,0:T(8,128)(2,1)} %rows.5), channel_id=1, source_target_pairs={{0,3},{1,2},{2,1},{3,0},{4,7},{5,6},{6,5},{7,4},{8,11},{9,10},{10,... | collective-permute-start | bytes 2359304 | tf_op jit(solution)/shard_map/ppermute | solution.py:544
  253.5 27.0 %collective-permute-start.42 = (bf16[128,3072]{1,0:T(8,128)(2,1)}, bf16[128,3072]{1,0:T(8,128)(2,1)}, u32[]{:S(2)}, u32[]{:S(2)}) collective-permute-start(bf16[128,3072]{1,0:T(8,128)(2,1)} %rows.4), channel_id=1, source_target_pairs={{0,2},{1,3},{2,0},{3,1},{4,6},{5,7},{6,4},{7,5},{8,10},{9,11},{10,... | collective-permute-start | bytes 2359304 | tf_op jit(solution)/shard_map/ppermute | solution.py:544
  276.7 25.5 %collective-permute-start.33 = (bf16[3,128,512]{2,1,0:T(8,128)(2,1)}, bf16[3,128,512]{2,1,0:T(8,128)(2,1)}, u32[]{:S(2)}, u32[]{:S(2)}) collective-permute-start(bf16[3,128,512]{2,1,0:T(8,128)(2,1)} %collective-permute-done.32.rest_5_), channel_id=1, source_target_pairs={{8,0},{16,8},{24,16},{28,24},{20,28},{12,20},{4,12},{0,4},{9,1},{1... | collective-permute-start | bytes 1179656 | tf_op jit(solution)/shard_map/ppermute | solution.py:579
  280.5 26.2 %collective-permute-start.23 = (bf16[3,128,512]{2,1,0:T(8,128)(2,1)}, bf16[3,128,512]{2,1,0:T(8,128)(2,1)}, u32[]{:S(2)}, u32[]{:S(2)}) collective-permute-start(bf16[3,128,512]{2,1,0:T(8,128)(2,1)} %collective-permute-done.22.rest_2_), channel_id=1, source_target_pairs={{0,8},{8,16},{16,24},{24,28},{28,20},{20,12},{12,4},{4,0},{1,9},{9... | collective-permute-start | bytes 1179656 | tf_op jit(solution)/shard_map/ppermute | solution.py:579
  299.0 74.5 %collective-permute-start.65 = (bf16[3,384,512]{2,1,0:T(8,128)(2,1)}, bf16[3,384,512]{2,1,0:T(8,128)(2,1)}, u32[]{:S(2)}, u32[]{:S(2)}) collective-permute-start(bf16[3,384,512]{2,1,0:T(8,128)(2,1)} %give.7), channel_id=1, source_target_pairs={{0,8},{8,16},{16,24},{24,28},{28,20},{20,12},{12,4},{4,0},{1,9},{9... | collective-permute-start | bytes 3538952 | tf_op jit(solution)/shard_map/ppermute | solution.py:579
  299.6 78.6 %collective-permute-start.56 = (bf16[3,384,512]{2,1,0:T(8,128)(2,1)}, bf16[3,384,512]{2,1,0:T(8,128)(2,1)}, u32[]{:S(2)}, u32[]{:S(2)}) collective-permute-start(bf16[3,384,512]{2,1,0:T(8,128)(2,1)} %give.6), channel_id=1, source_target_pairs={{8,0},{16,8},{24,16},{28,24},{20,28},{12,20},{4,12},{0,4},{9,1},{1... | collective-permute-start | bytes 3538952 | tf_op jit(solution)/shard_map/ppermute | solution.py:579
  302.3 67.4 %collective-permute-start.44 = (bf16[4,384,256]{2,1,0:T(8,128)(2,1)}, bf16[4,384,256]{2,1,0:T(8,128)(2,1)}, u32[]{:S(2)}, u32[]{:S(2)}) collective-permute-start(bf16[4,384,256]{2,1,0:T(8,128)(2,1)} %fusion), channel_id=1, source_target_pairs={{0,4},{4,0},{8,12},{12,8},{16,20},{20,16},{24,28},{28,24},{1,5},{5... | collective-permute-start | bytes 2359304 | tf_op jit(solution)/shard_map/ppermute | solution.py:544
  306.7 36.9 %collective-permute-start.8 = (f32[8,128]{1,0:T(8,128)}, f32[8,128]{1,0:T(8,128)}, u32[]{:S(2)}, u32[]{:S(2)}) collective-permute-start(f32[8,128]{1,0:T(8,128)} %copy-done.9), channel_id=1, source_target_pairs={{0,4},{4,0},{8,12},{12,8},{16,20},{20,16},{24,28},{28,24},{1,5},{5... | collective-permute-start | bytes 12296 | tf_op jit(solution)/shard_map/ppermute | solution.py:544
  307.8 37.7 %collective-permute-start.9 = (f32[8,128]{1,0:T(8,128)}, f32[8,128]{1,0:T(8,128)}, u32[]{:S(2)}, u32[]{:S(2)}) collective-permute-start(f32[8,128]{1,0:T(8,128)} %copy-done.9), channel_id=1, source_target_pairs={{0,8},{4,12},{8,0},{12,4},{16,24},{20,28},{24,16},{28,20},{1,9},{5... | collective-permute-start | bytes 12296 | tf_op jit(solution)/shard_map/ppermute | solution.py:544
  343.6 53.1 %collective-permute-start.40 = (bf16[3,384,512]{2,1,0:T(8,128)(2,1)}, bf16[3,384,512]{2,1,0:T(8,128)(2,1)}, u32[]{:S(2)}, u32[]{:S(2)}) collective-permute-start(bf16[3,384,512]{2,1,0:T(8,128)(2,1)} %give.5), channel_id=1, source_target_pairs={{8,0},{16,8},{24,16},{28,24},{20,28},{12,20},{4,12},{0,4},{9,1},{1... | collective-permute-start | bytes 3538952 | tf_op jit(solution)/shard_map/ppermute | solution.py:579
  345.5 51.2 %collective-permute-start.27 = (bf16[3,384,512]{2,1,0:T(8,128)(2,1)}, bf16[3,384,512]{2,1,0:T(8,128)(2,1)}, u32[]{:S(2)}, u32[]{:S(2)}) collective-permute-start(bf16[3,384,512]{2,1,0:T(8,128)(2,1)} %give.4), channel_id=1, source_target_pairs={{0,8},{8,16},{16,24},{24,28},{28,20},{20,12},{12,4},{4,0},{1,9},{9... | collective-permute-start | bytes 3538952 | tf_op jit(solution)/shard_map/ppermute | solution.py:579
  (49 other events, 978.2 us)
where the time goes:
time: 402 us; the launch traced here: 401 us
  waiting for transfers between devices  154 us (38%)
  Pallas kernels  152 us (38%)
  starting transfers between devices  84.3 us (21%)
  local copies, waits for them, and re-layouts  4.9 us (1%)
    ppermute x19, waiting for transfers between devices, swap(): return lax.ppermute(value, axis, [(i, i ^ bit) for i in range(size)])  79 us
    ppermute x44, waiting for transfers between devices, pass_on(): return lax.ppermute(value, 'dp', right if way == 'r' else left)  75 us
    ppermute x44, starting transfers between devices, pass_on(): return lax.ppermute(value, 'dp', right if way == 'r' else left)  54.5 us
    pallas_call x7, Pallas kernels, clipped_rows(): pl.pallas_call(body, out_shape=jax.ShapeDtypeStruct((3, rows, 2 * half *...  35.7 us
    pallas_call x4, Pallas kernels, expert_units(): pl.pallas_call(body, out_shape=[jax.ShapeDtypeStruct((3, slots, half), BF...  33.6 us
    pallas_call x3, Pallas kernels, row_gradients(): pl.pallas_call(body, out_shape=[jax.ShapeDtypeStruct((CAP, width), BF16)]...  25.2 us
    ppermute x19, starting transfers between devices, swap(): return lax.ppermute(value, axis, [(i, i ^ bit) for i in range(size)])  24.2 us
    pallas_call x1, Pallas kernels, square_sum(): pl.pallas_call(body, out_shape=[jax.ShapeDtypeStruct((8, 128), F32)] + [j...  18.2 us
  transfers between devices with their start and end apart: 66, of which 23 were waited for; matrix products, arithmetic and copies ran while one was open for 2% of the time, Pallas kernels for 35%

commit v1 on v0

--- a/solution.py
+++ b/solution.py
@@ -383,7 +383,7 @@
     )
 
 
-def clipped_rows(ids, scale, x_own, w_own, groups, out, owner, shards, only=None):
+def clipped_rows(ids, scale, x_own, w_own, groups, out, owner, shards, given=None, at=0):
     rows, slots = x_own.shape
     half = groups[0][0].shape[2]
     number = len(groups[0])
@@ -391,18 +391,23 @@
     operands = [ids, scale, x_own, w_own, *flat(groups)]
     specs = [pl.BlockSpec(memory_space=pltpu.SMEM)]
     specs += [pl.BlockSpec((rows, slots), lambda j, ids: (0, 0))] * 2 + held(flat(groups))
+    if given is not None:
+        operands.append(given)
+        specs += held([given])
 
     def body(ids_ref, scale_ref, x_ref, w_ref, *rest):
+        def store(h, k, grads):
+            clipped = (grads.astype(F32) * scale_ref[0, 0]).astype(BF16)
+            rest[-1][k, :, h * half : (h + 1) * half] = clipped
+
         for h in range(halves):
             part = rest[h * number : (h + 1) * number]
             for k, grads in gradient_rows(x_ref, w_ref, part):
-                clipped = (grads.astype(F32) * scale_ref[0, 0]).astype(BF16)
-                rest[-1][k, :, h * half : (h + 1) * half] = clipped
-
-    if only is None:
-        column = lambda j, ids: (0, 0, owner(ids[0]))
-    else:
-        column = lambda j, ids: (0, 0, owner(ids[0]) * 2 + only)
+                store(at + h, k, grads)
+        if given is not None:
+            for k in range(3):
+                store(1 - at, k, rest[number][k])
+
     aliases = {}
     if out is not None:
         aliases = {len(operands): 0}
@@ -415,7 +420,9 @@
             num_scalar_prefetch=1,
             grid=(1,),
             in_specs=specs,
-            out_specs=pl.BlockSpec((3, rows, halves * half), column),
+            out_specs=pl.BlockSpec(
+                (3, rows, 2 * half), lambda j, ids: (0, 0, owner(ids[0]))
+            ),
         ),
         input_output_aliases=aliases,
         compiler_params=params(),
@@ -503,31 +510,67 @@
     )(*operands)
 
 
-def token_sums(tiles, picks):
+def token_sums(ids, tiles, picks, shards):
     number = len(tiles)
     width = tiles[0].shape[1]
     count = picks[0].shape[1]
-    tn = tile_of(width, 768, 128)
-
-    def body(*refs):
-        rows, pick = stacked(refs[:number]), stacked(refs[number : 2 * number])
-        refs[2 * number][...] = dot_tn(rows, pick)
-
+    rows = width // shards
+    half = shards // 2
+    cost = pl.CostEstimate(
+        flops=2 * number * CAP * width * count,
+        bytes_accessed=2 * number * CAP * width + 3 * width * count,
+        transcendentals=0,
+    )
+    if rows % 128:
+        tn = tile_of(width, 768, 128)
+
+        def whole(*refs):
+            rows_in, pick = stacked(refs[:number]), stacked(refs[number : 2 * number])
+            refs[2 * number][...] = dot_tn(rows_in, pick)
+
+        partial = pl.pallas_call(
+            whole,
+            out_shape=jax.ShapeDtypeStruct((width, count), F32),
+            grid=(width // tn,),
+            in_specs=[pl.BlockSpec((CAP, tn), lambda j: (0, j))] * number
+            + [pl.BlockSpec((CAP, count), lambda j: (0, 0))] * number,
+            out_specs=pl.BlockSpec((tn, count), lambda j: (j, 0)),
+            compiler_params=params(),
+            cost_estimate=cost,
+            name="combine",
+        )(*tiles, *picks).reshape(half, 2, rows, count)
+        inner = ids[0] % 2
+        keep = lax.dynamic_index_in_dim(partial, inner, 1, keepdims=False)
+        send = lax.dynamic_index_in_dim(partial, 1 - inner, 1, keepdims=False)
+        return keep, send.astype(BF16)
+
+    def body(ids_ref, *refs):
+        mine, other = stacked(refs[:number]), stacked(refs[number : 2 * number])
+        pick = stacked(refs[2 * number : 3 * number])
+        keep_ref, send_ref = refs[3 * number :]
+        keep_ref[0] = dot_tn(mine, pick)
+        send_ref[0] = dot_tn(other, pick).astype(BF16)
+
+    mine = pl.BlockSpec((CAP, rows), lambda j, ids: (0, 2 * j + ids[0] % 2))
+    other = pl.BlockSpec((CAP, rows), lambda j, ids: (0, 2 * j + 1 - ids[0] % 2))
+    pick = pl.BlockSpec((CAP, count), lambda j, ids: (0, 0))
+    block = pl.BlockSpec((1, rows, count), lambda j, ids: (j, 0, 0))
     return pl.pallas_call(
         body,
-        out_shape=jax.ShapeDtypeStruct((width, count), F32),
-        grid=(width // tn,),
-        in_specs=[pl.BlockSpec((CAP, tn), lambda j: (0, j))] * number
-        + [pl.BlockSpec((CAP, count), lambda j: (0, 0))] * number,
-        out_specs=pl.BlockSpec((tn, count), lambda j: (j, 0)),
-        compiler_params=params(),
-        cost_estimate=pl.CostEstimate(
-            flops=2 * number * CAP * width * count,
-            bytes_accessed=2 * number * CAP * width + 4 * width * count,
-            transcendentals=0,
-        ),
+        out_shape=[
+            jax.ShapeDtypeStruct((half, rows, count), F32),
+            jax.ShapeDtypeStruct((half, rows, count), BF16),
+        ],
+        grid_spec=pltpu.PrefetchScalarGridSpec(
+            num_scalar_prefetch=1,
+            grid=(half,),
+            in_specs=[mine] * number + [other] * number + [pick] * number,
+            out_specs=[block, block],
+        ),
+        compiler_params=params(),
+        cost_estimate=cost,
         name="combine",
-    )(*tiles, *picks)
+    )(ids, *tiles, *tiles, *picks)
 
 
 def per_device(tokens, cotangent, routes, gate_values, gate_weight, up_weight, down_weight):
@@ -622,10 +665,8 @@
     back = sent[:1]
     for r in range(1, experts):
         back.append(swap(sent[r], "expert", experts, r))
-    outer, inner = ids[0] // 2, ids[0] % 2
-    partial = token_sums(back, picks).reshape(half, 2, rows, tokens.shape[0])
-    send = lax.dynamic_index_in_dim(partial, 1 - inner, 1, keepdims=False).astype(BF16)
-    keep = lax.dynamic_index_in_dim(partial, inner, 1, keepdims=False)
+    outer = ids[0] // 2
+    keep, send = token_sums(ids, back, picks, shards)
     other = swap(send, "dp", shards, 1)
     sums = keep + other.astype(F32)
     parts = []
@@ -638,11 +679,10 @@
     for step in clip_order(shards):
         groups = [half_of(chunks[step], h) for h in range(2)]
         out = clipped_rows(*common, groups, out, owner_at(step), shards)
-    for h, step, parts_at in ((0, half - 1, from_left), (1, half + 1, from_right)):
+    sides = ((0, half - 1, from_left, right_b), (1, half + 1, from_right, left_a))
+    for h, step, parts_at, given in sides:
         group = [half_of(parts_at, h)]
-        out = clipped_rows(*common, group, out, owner_at(step), shards, only=h)
-    owners = (owner_at(half + 1), owner_at(half - 1))
-    (out,) = placed_rows(ids, scale, left_a, right_b, out, owners)
+        out = clipped_rows(*common, group, out, owner_at(step), shards, given, h)
     owners = (owner_at(half), owner_at(half))
     out, d_tokens = placed_rows(ids, scale, right_a, left_b, out, owners, (sums, parts))
     return (out[None], d_tokens)

time: 402 us -> 401 us (level)
  waiting for transfers between devices: 154 us -> 166 us
  starting transfers between devices: 84.3 us -> 74 us
    ppermute x44, waiting for transfers between devices: 75 us -> 83.1 us  [pass_on(): return lax.ppermute(value, 'dp', right if way == 'r' else left)]
    ppermute x19, starting transfers between devices: 24.2 us -> 18.8 us  [swap(): return lax.ppermute(value, axis, [(i, i ^ bit) for i in range(size)])]
    pallas_call x2 -> x1, Pallas kernels: 8.38 us -> 4.42 us  [placed_rows(): pl.pallas_call(body, out_shape=out_shape, grid_spec=pltpu.PrefetchScalarG...]
  transfers between devices with their start and end apart: 66 -> 66, of which waited for: 23 -> 26; matrix products, arithmetic and copies ran while one was open for 2% -> 1% of each run, Pallas kernels for 35% -> 35%
where the time goes in v1:
time: 401 us; the launch traced here: 400 us
  waiting for transfers between devices  166 us (41%)
  Pallas kernels  151 us (38%)
  starting transfers between devices  74 us (18%)
    ppermute x44, waiting for transfers between devices, pass_on(): return lax.ppermute(value, 'dp', right if way == 'r' else left)  83.1 us
    ppermute x19, waiting for transfers between devices, swap(): return lax.ppermute(value, axis, [(i, i ^ bit) for i in range(size)])  82.6 us
    ppermute x44, starting transfers between devices, pass_on(): return lax.ppermute(value, 'dp', right if way == 'r' else left)  51.3 us
    pallas_call x7, Pallas kernels, clipped_rows(): pl.pallas_call(body, out_shape=jax.ShapeDtypeStruct((3, rows, 2 * half *...  38 us
    pallas_call x4, Pallas kernels, expert_units(): pl.pallas_call(body, out_shape=[jax.ShapeDtypeStruct((3, slots, half), BF...  33.9 us
    pallas_call x3, Pallas kernels, row_gradients(): pl.pallas_call(body, out_shape=[jax.ShapeDtypeStruct((CAP, width), BF16)]...  25.2 us
    ppermute x19, starting transfers between devices, swap(): return lax.ppermute(value, axis, [(i, i ^ bit) for i in range(size)])  18.8 us
    pallas_call x1, Pallas kernels, square_sum(): pl.pallas_call(body, out_shape=[jax.ShapeDtypeStruct((8, 128), F32)] + [j...  18.2 us
  transfers between devices with their start and end apart: 66, of which 26 were waited for; matrix products, arithmetic and copies ran while one was open for 1% of the time, Pallas kernels for 35%

profile of v1, /device:TPU:0, one launch (start us, length us, event | category | flops | bytes accessed | tf_op | source)
XLA Modules:
  0.0 400.3 jit_solution(4617606417396512404)
XLA Ops:
  0.6 7.9 %first.1 = (bf16[3,128,512]{2,1,0:T(8,128)(2,1)}, bf16[128,3072]{1,0:T(8,128)(2,1)}, bf16[128,3072]{1,0:T(8,128)(2,1)}, bf16[128,3072]{1,0:T(8,128)(2,1)}, bf16[...) custom-call(s32[2,256]{1,0:T(2,128)} %bitcast.36, bf16[2,256]{1,0:T(2,128)(2,1)} %bitcast.38, ...), custom_call_target="tpu_custom_call" | custom-call | flops 1207959552 | bytes 15728640 | tf_op jit(solution)/shard_map/first/pallas_call | solution.py:183
  17.3 5.7 %units.4.refs_5_.refs_9_.refs_1_.rest_4_ = bf16[3,128,512]{2,1,0:T(8,128)(2,1)} custom-call(bf16[128,3072]{1,0:T(8,128)(2,1)} %get-tuple-element.34.refs_0_, bf16[128,3072]{1,0:T(8,128)(2,1)} %get-tuple-element.38.refs_1_.refs_4_, bf16[3072,1024]{1,0:T(8,128)(2,1)} %bitcast.16, bf16[3072,1024]{1,0:T(8,128)(2,1)} %bitcast.24, bf16[3072,1024]{1,0:T(8,128)(2,1)} %bitcast.32, ...), custom_call_target="tpu_custom_call" | custom-call | flops 1207959552 | bytes 10616832 | tf_op jit(solution)/shard_map/units/pallas_call | solution.py:232
  25.1 9.1 %collective-permute-done.57.rest_4_ = bf16[3,128,512]{2,1,0:T(8,128)(2,1)} collective-permute-done((bf16[3,128,512]{2,1,0:T(8,128)(2,1)}, bf16[3,128,512]{2,1,0:T(8,128)(2,1)}, u32[]{:S(2)}, u32[]{:S(2)}) %collective-permute-start.57) | collective-permute-done | bytes 393248 | tf_op jit(solution)/shard_map/ppermute | solution.py:622
  38.0 14.8 %collective-permute-done.4.refs_1_.refs_6_ = bf16[128,3072]{1,0:T(8,128)(2,1)} collective-permute-done((bf16[128,3072]{1,0:T(8,128)(2,1)}, bf16[128,3072]{1,0:T(8,128)(2,1)}, u32[]{:S(2)}, u32[]{:S(2)}) %collective-permute-start.4) | collective-permute-done | bytes 786464 | tf_op jit(solution)/shard_map/ppermute | solution.py:587
  54.8 9.4 %units.5 = (bf16[3,128,512]{2,1,0:T(8,128)(2,1)}, bf16[3,128,512]{2,1,0:T(8,128)(2,1)}) custom-call(bf16[128,3072]{1,0:T(8,128)(2,1)} %collective-permute-done.refs_0_.refs_1_, bf16[128,3072]{1,0:T(8,128)(2,1)} %collective-permute-done.3.refs_1_.refs_5_, bf16[3072,1024]{1,0:T(8,128)(2,1)} %bitcast.17, bf16[3072,1024]{1,0:T(8,128)(2,1)} %bitcast.25, ...), custom_call_target="tpu_custom_call" | custom-call | flops 2415919104 | bytes 21233664 | tf_op jit(solution)/shard_map/units/pallas_call | solution.py:232
  64.2 9.5 %units.6 = (bf16[3,128,512]{2,1,0:T(8,128)(2,1)}, bf16[3,128,512]{2,1,0:T(8,128)(2,1)}) custom-call(bf16[128,3072]{1,0:T(8,128)(2,1)} %collective-permute-done.1.refs_0_.refs_2_, bf16[128,3072]{1,0:T(8,128)(2,1)} %collective-permute-done.4.refs_1_.refs_6_, bf16[3072,1024]{1,0:T(8,128)(2,1)} %bitcast.18, bf16[3072,1024]{1,0:T(8,128)(2,1)} %bitcast.26, ...), custom_call_target="tpu_custom_call" | custom-call | flops 2415919104 | bytes 21233664 | tf_op jit(solution)/shard_map/units/pallas_call | solution.py:232
  77.8 7.5 %collective-permute-done.5.refs_1_.refs_7_ = bf16[128,3072]{1,0:T(8,128)(2,1)} collective-permute-done((bf16[128,3072]{1,0:T(8,128)(2,1)}, bf16[128,3072]{1,0:T(8,128)(2,1)}, u32[]{:S(2)}, u32[]{:S(2)}) %collective-permute-start.5) | collective-permute-done | bytes 786464 | tf_op jit(solution)/shard_map/ppermute | solution.py:587
  85.3 9.3 %units.7 = (bf16[3,128,512]{2,1,0:T(8,128)(2,1)}, bf16[3,128,512]{2,1,0:T(8,128)(2,1)}) custom-call(bf16[128,3072]{1,0:T(8,128)(2,1)} %collective-permute-done.2.refs_0_.refs_3_, bf16[128,3072]{1,0:T(8,128)(2,1)} %collective-permute-done.5.refs_1_.refs_7_, bf16[3072,1024]{1,0:T(8,128)(2,1)} %bitcast.19, bf16[3072,1024]{1,0:T(8,128)(2,1)} %bitcast.27, ...), custom_call_target="tpu_custom_call" | custom-call | flops 2415919104 | bytes 21233664 | tf_op jit(solution)/shard_map/units/pallas_call | solution.py:232
  94.6 18.2 %squares.1 = (f32[8,128]{1,0:T(8,128)}, bf16[384,512]{1,0:T(8,128)(2,1)}, bf16[384,512]{1,0:T(8,128)(2,1)}, bf16[384,512]{1,0:T(8,128)(2,1)}, bf16[384,512]{1,0:...) custom-call(s32[2]{0:T(128)} %pad_add_fusion.ids_ref, bf16[128,3072]{1,0:T(8,128)(2,1)} %get-tuple-element.34.refs_0_, ...), custom_call_target="tpu_custom_call" | custom-call | flops 9663676416 | bytes 9437184 | tf_op jit(solution)/shard_map/squares/pallas_call | solution.py:322
  124.9 26.6 %collective-permute-done.10 = f32[8,128]{1,0:T(8,128)S(1)} collective-permute-done((f32[8,128]{1,0:T(8,128)S(1)}, f32[8,128]{1,0:T(8,128)S(1)}, u32[]{:S(2)}, u32[]{:S(2)}) %collective-permute-start.10) | collective-permute-done | bytes 4128 | tf_op jit(solution)/shard_map/ppermute | solution.py:587
  156.0 5.4 %collective-permute-done.12 = f32[8,128]{1,0:T(8,128)S(1)} collective-permute-done((f32[8,128]{1,0:T(8,128)S(1)}, f32[8,128]{1,0:T(8,128)S(1)}, u32[]{:S(2)}, u32[]{:S(2)}) %collective-permute-start.12) | collective-permute-done | bytes 4128 | tf_op jit(solution)/shard_map/ppermute | solution.py:587
  161.5 5.4 %collective-permute-done.13 = f32[8,128]{1,0:T(8,128)S(1)} collective-permute-done((f32[8,128]{1,0:T(8,128)S(1)}, f32[8,128]{1,0:T(8,128)S(1)}, u32[]{:S(2)}, u32[]{:S(2)}) %collective-permute-start.13) | collective-permute-done | bytes 4128 | tf_op jit(solution)/shard_map/ppermute | solution.py:587
  177.8 5.2 %collective-permute-done.59.rest_5_ = bf16[3,128,512]{2,1,0:T(8,128)(2,1)} collective-permute-done((bf16[3,128,512]{2,1,0:T(8,128)(2,1)}, bf16[3,128,512]{2,1,0:T(8,128)(2,1)}, u32[]{:S(2)}, u32[]{:S(2)}) %collective-permute-start.59) | collective-permute-done | bytes 393248 | tf_op jit(solution)/shard_map/ppermute | solution.py:622
  187.9 6.5 %collective-permute-done.54.rest_3_ = bf16[3,128,512]{2,1,0:T(8,128)(2,1)S(1)} collective-permute-done((bf16[3,128,512]{2,1,0:T(8,128)(2,1)}, bf16[3,128,512]{2,1,0:T(8,128)(2,1)S(1)}, u32[]{:S(2)}, u32[]{:S(2)}) %collective-permute-start.54) | collective-permute-done | bytes 393248 | tf_op jit(solution)/shard_map/ppermute | solution.py:622
  196.0 6.8 %collective-permute-done.34.rest_6_ = bf16[3,128,512]{2,1,0:T(8,128)(2,1)S(1)} collective-permute-done((bf16[3,128,512]{2,1,0:T(8,128)(2,1)}, bf16[3,128,512]{2,1,0:T(8,128)(2,1)S(1)}, u32[]{:S(2)}, u32[]{:S(2)}) %collective-permute-start.34) | collective-permute-done | bytes 393248 | tf_op jit(solution)/shard_map/ppermute | solution.py:622
  205.7 5.6 %collective-permute-done.52.rest_2_ = bf16[3,128,512]{2,1,0:T(8,128)(2,1)S(1)} collective-permute-done((bf16[3,128,512]{2,1,0:T(8,128)(2,1)}, bf16[3,128,512]{2,1,0:T(8,128)(2,1)S(1)}, u32[]{:S(2)}, u32[]{:S(2)}) %collective-permute-start.52) | collective-permute-done | bytes 393248 | tf_op jit(solution)/shard_map/ppermute | solution.py:622
  214.1 5.6 %collective-permute-done.31.rest_5_ = bf16[3,128,512]{2,1,0:T(8,128)(2,1)S(1)} collective-permute-done((bf16[3,128,512]{2,1,0:T(8,128)(2,1)}, bf16[3,128,512]{2,1,0:T(8,128)(2,1)S(1)}, u32[]{:S(2)}, u32[]{:S(2)}) %collective-permute-start.31) | collective-permute-done | bytes 393248 | tf_op jit(solution)/shard_map/ppermute | solution.py:622
  235.0 8.4 %rows.5 = bf16[128,3072]{1,0:T(8,128)(2,1)} custom-call(bf16[3,128,512]{2,1,0:T(8,128)(2,1)} %get-tuple-element.47.refs_14_.refs_0_.rest_3_, bf16[3,128,512]{2,1,0:T(8,128)(2,1)} %get-tuple-element.48.refs_15_.refs_1_.rest_7_, bf16[3072,1024]{1,0:T(8,128)(2,1)} %bitcast.20, bf16[3072,1024]{1,0:T(8,128)(2,1)} %bitcast.28), custom_call_target="tpu_custom_call" | custom-call | flops 1610612736 | bytes 14155776 | tf_op jit(solution)/shard_map/rows/pallas_call | solution.py:267
  246.3 8.3 %rows.3 = (bf16[128,3072]{1,0:T(8,128)(2,1)}, bf16[128,3072]{1,0:T(8,128)(2,1)}) custom-call(bf16[3,128,512]{2,1,0:T(8,128)(2,1)} %get-tuple-element.42.refs_5_.refs_8_.refs_0_.rest_0_, bf16[3,128,512]{2,1,0:T(8,128)(2,1)} %units.4.refs_5_.refs_9_.refs_1_.rest_4_, bf16[3,128,512]{2,1,0:T(8,128)(2,1)} %get-tuple-element.43.refs_10_.refs_2_.rest_1_, ...), custom_call_target="tpu_custom_call" | custom-call | flops 3221225472 | bytes 15728640 | tf_op jit(solution)/shard_map/rows/pallas_call | solution.py:267
  254.7 8.4 %rows.4 = bf16[128,3072]{1,0:T(8,128)(2,1)} custom-call(bf16[3,128,512]{2,1,0:T(8,128)(2,1)} %get-tuple-element.45.refs_12_.refs_0_.rest_2_, bf16[3,128,512]{2,1,0:T(8,128)(2,1)} %get-tuple-element.46.refs_5_.refs_13_.refs_1_.rest_6_, bf16[3072,1024]{1,0:T(8,128)(2,1)} %bitcast.22, bf16[3072,1024]{1,0:T(8,128)(2,1)} %bitcast.30), custom_call_target="tpu_custom_call" | custom-call | flops 1610612736 | bytes 14155776 | tf_op jit(solution)/shard_map/rows/pallas_call | solution.py:267
  268.5 8.1 %collective-permute-done.53.rest_2_ = bf16[3,128,512]{2,1,0:T(8,128)(2,1)} collective-permute-done((bf16[3,128,512]{2,1,0:T(8,128)(2,1)}, bf16[3,128,512]{2,1,0:T(8,128)(2,1)}, u32[]{:S(2)}, u32[]{:S(2)}) %collective-permute-start.53) | collective-permute-done | bytes 393248 | tf_op jit(solution)/shard_map/ppermute | solution.py:622
  276.7 8.4 %collective-permute-done.32.rest_5_ = bf16[3,128,512]{2,1,0:T(8,128)(2,1)} collective-permute-done((bf16[3,128,512]{2,1,0:T(8,128)(2,1)}, bf16[3,128,512]{2,1,0:T(8,128)(2,1)}, u32[]{:S(2)}, u32[]{:S(2)}) %collective-permute-start.32) | collective-permute-done | bytes 393248 | tf_op jit(solution)/shard_map/ppermute | solution.py:622
  285.1 8.4 %collective-permute-done.51.rest_1_ = bf16[3,128,512]{2,1,0:T(8,128)(2,1)} collective-permute-done((bf16[3,128,512]{2,1,0:T(8,128)(2,1)}, bf16[3,128,512]{2,1,0:T(8,128)(2,1)}, u32[]{:S(2)}, u32[]{:S(2)}) %collective-permute-start.51) | collective-permute-done | bytes 393248 | tf_op jit(solution)/shard_map/ppermute | solution.py:622
  303.4 6.8 %collective-permute-done.36.rest_2_ = bf16[3,128,512]{2,1,0:T(8,128)(2,1)} collective-permute-done((bf16[3,128,512]{2,1,0:T(8,128)(2,1)}, bf16[3,128,512]{2,1,0:T(8,128)(2,1)}, u32[]{:S(2)}, u32[]{:S(2)}) %collective-permute-start.36) | collective-permute-done | bytes 393248 | tf_op jit(solution)/shard_map/ppermute | solution.py:622
  316.9 5.6 %combine.1 = (f32[4,384,256]{2,1,0:T(8,128)}, bf16[4,384,256]{2,1,0:T(8,128)(2,1)}) custom-call(s32[2]{0:T(128)} %pad_add_fusion.ids_ref, bf16[128,3072]{1,0:T(8,128)(2,1)} %get-tuple-element.54.refs_0_.refs_4_, bf16[128,3072]{1,0:T(8,128)(2,1)} %collective-permute-done.41.refs_1_.refs_5_, bf16[128,3072]{1,0:T(8,128)(2,1)} %collective-permute-done.42.refs_2_.refs_6_, ...), custom_call_target="tpu_custom_call" | custom-call | flops 805306368 | bytes 5505024 | tf_op jit(solution)/shard_map/combine/pallas_call | solution.py:558
  334.5 11.7 %collective-permute-done.8 = f32[8,128]{1,0:T(8,128)} collective-permute-done((f32[8,128]{1,0:T(8,128)}, f32[8,128]{1,0:T(8,128)}, u32[]{:S(2)}, u32[]{:S(2)}) %collective-permute-start.8) | collective-permute-done | bytes 4128 | tf_op jit(solution)/shard_map/ppermute | solution.py:587
  350.2 5.5 %clip.7.rest_8_ = bf16[3,384,8192]{2,1,0:T(8,128)(2,1)} custom-call(s32[2]{0:T(128)} %pad_add_fusion.ids_ref, f32[1,1]{1,0:T(1,128)S(6)} %div.11.scale_ref, bf16[384,512]{1,0:T(8,128)(2,1)} %get-tuple-element.62.x_ref, bf16[384,512]{1,0:T(8,128)(2,1)} %get-tuple-element.63.w_ref, bf16[3,128,512]{2,1,0:T(8,128)(2,1)} %get-tuple-element.42.refs_5_.refs_8_.refs_0_.rest_0_, ...), custom_call_target="tpu_custom_call" | custom-call | flops 1207959552 | bytes 6291456 | tf_op jit(solution)/shard_map/clip/pallas_call | solution.py:416
  355.7 5.5 %clip.8.rest_8_ = bf16[3,384,8192]{2,1,0:T(8,128)(2,1)} custom-call(s32[2]{0:T(128)} %pad_add_fusion.ids_ref, f32[1,1]{1,0:T(1,128)S(6)} %div.11.scale_ref, bf16[384,512]{1,0:T(8,128)(2,1)} %get-tuple-element.62.x_ref, bf16[384,512]{1,0:T(8,128)(2,1)} %get-tuple-element.63.w_ref, ...), custom_call_target="tpu_custom_call", output_to_operand_aliasing={{}: (12, {})} | custom-call | flops 1207959552 | bytes 6291456 | tf_op jit(solution)/shard_map/clip/pallas_call | solution.py:416
  361.3 5.5 %clip.9.rest_8_ = bf16[3,384,8192]{2,1,0:T(8,128)(2,1)} custom-call(s32[2]{0:T(128)} %pad_add_fusion.ids_ref, f32[1,1]{1,0:T(1,128)S(6)} %div.11.scale_ref, bf16[384,512]{1,0:T(8,128)(2,1)} %get-tuple-element.62.x_ref, bf16[384,512]{1,0:T(8,128)(2,1)} %get-tuple-element.63.w_ref, ...), custom_call_target="tpu_custom_call", output_to_operand_aliasing={{}: (12, {})} | custom-call | flops 1207959552 | bytes 6291456 | tf_op jit(solution)/shard_map/clip/pallas_call | solution.py:416
  366.8 5.5 %clip.10.rest_8_ = bf16[3,384,8192]{2,1,0:T(8,128)(2,1)} custom-call(s32[2]{0:T(128)} %pad_add_fusion.ids_ref, f32[1,1]{1,0:T(1,128)S(6)} %div.11.scale_ref, bf16[384,512]{1,0:T(8,128)(2,1)} %get-tuple-element.62.x_ref, bf16[384,512]{1,0:T(8,128)(2,1)} %get-tuple-element.63.w_ref, ...), custom_call_target="tpu_custom_call", output_to_operand_aliasing={{}: (12, {})} | custom-call | flops 1207959552 | bytes 6291456 | tf_op jit(solution)/shard_map/clip/pallas_call | solution.py:416
  379.9 5.5 %clip.11.rest_5_ = bf16[3,384,8192]{2,1,0:T(8,128)(2,1)} custom-call(s32[2]{0:T(128)} %pad_add_fusion.ids_ref, f32[1,1]{1,0:T(1,128)S(6)} %div.11.scale_ref, bf16[384,512]{1,0:T(8,128)(2,1)} %get-tuple-element.62.x_ref, bf16[384,512]{1,0:T(8,128)(2,1)} %get-tuple-element.63.w_ref, ...), custom_call_target="tpu_custom_call", output_to_operand_aliasing={{}: (12, {})} | custom-call | flops 1207959552 | bytes 6291456 | tf_op jit(solution)/shard_map/clip/pallas_call | solution.py:416
  385.5 5.2 %clip.12.rest_5_ = bf16[3,384,8192]{2,1,0:T(8,128)(2,1)} custom-call(s32[2]{0:T(128)} %pad_add_fusion.ids_ref, f32[1,1]{1,0:T(1,128)S(6)} %div.11.scale_ref, bf16[384,512]{1,0:T(8,128)(2,1)} %get-tuple-element.62.x_ref, bf16[384,512]{1,0:T(8,128)(2,1)} %get-tuple-element.63.w_ref, ...), custom_call_target="tpu_custom_call", output_to_operand_aliasing={{}: (9, {})} | custom-call | flops 603979776 | bytes 3145728 | tf_op jit(solution)/shard_map/clip/pallas_call | solution.py:416
  (160 shorter events, 133.0 us)
Async XLA Ops:
  17.2 35.6 %collective-permute-start.4 = (bf16[128,3072]{1,0:T(8,128)(2,1)}, bf16[128,3072]{1,0:T(8,128)(2,1)}, u32[]{:S(2)}, u32[]{:S(2)}) collective-permute-start(bf16[128,3072]{1,0:T(8,128)(2,1)} %get-tuple-element.40), channel_id=1, source_target_pairs={{0,2},{1,3},{2,0},{3,1},{4,6},{5,7},{6,4},{7,5},{8,10},{9,11},{10,... | collective-permute-start | bytes 2359304 | tf_op jit(solution)/shard_map/ppermute | solution.py:587
  34.2 41.6 %collective-permute-start.2 = (bf16[128,3072]{1,0:T(8,128)(2,1)}, bf16[128,3072]{1,0:T(8,128)(2,1)}, u32[]{:S(2)}, u32[]{:S(2)}) collective-permute-start(bf16[128,3072]{1,0:T(8,128)(2,1)} %get-tuple-element.37), channel_id=1, source_target_pairs={{0,3},{1,2},{2,1},{3,0},{4,7},{5,6},{6,5},{7,4},{8,11},{9,10},{10,... | collective-permute-start | bytes 2359304 | tf_op jit(solution)/shard_map/ppermute | solution.py:587
  34.2 51.1 %collective-permute-start.5 = (bf16[128,3072]{1,0:T(8,128)(2,1)}, bf16[128,3072]{1,0:T(8,128)(2,1)}, u32[]{:S(2)}, u32[]{:S(2)}) collective-permute-start(bf16[128,3072]{1,0:T(8,128)(2,1)} %get-tuple-element.41), channel_id=1, source_target_pairs={{0,3},{1,2},{2,1},{3,0},{4,7},{5,6},{6,5},{7,4},{8,11},{9,10},{10,... | collective-permute-start | bytes 2359304 | tf_op jit(solution)/shard_map/ppermute | solution.py:587
  35.9 37.8 %collective-permute-start.15 = (bf16[3,128,512]{2,1,0:T(8,128)(2,1)}, bf16[3,128,512]{2,1,0:T(8,128)(2,1)}, u32[]{:S(2)}, u32[]{:S(2)}) collective-permute-start(bf16[3,128,512]{2,1,0:T(8,128)(2,1)} %get-tuple-element.42.refs_5_.refs_8_.refs_0_.rest_0_), channel_id=1, source_target_pairs={{0,8},{8,16},{16,24},{24,28},{28,20},{20,12},{12,4},{4,0},{1,9},{9... | collective-permute-start | bytes 1179656 | tf_op jit(solution)/shard_map/ppermute | solution.py:622
  37.7 36.1 %collective-permute-start.28 = (bf16[3,128,512]{2,1,0:T(8,128)(2,1)}, bf16[3,128,512]{2,1,0:T(8,128)(2,1)}, u32[]{:S(2)}, u32[]{:S(2)}) collective-permute-start(bf16[3,128,512]{2,1,0:T(8,128)(2,1)} %units.4.refs_5_.refs_9_.refs_1_.rest_4_), channel_id=1, source_target_pairs={{8,0},{16,8},{24,16},{28,24},{20,28},{12,20},{4,12},{0,4},{9,1},{1... | collective-permute-start | bytes 1179656 | tf_op jit(solution)/shard_map/ppermute | solution.py:622
  73.7 39.9 %collective-permute-start.58 = (bf16[3,128,512]{2,1,0:T(8,128)(2,1)}, bf16[3,128,512]{2,1,0:T(8,128)(2,1)}, u32[]{:S(2)}, u32[]{:S(2)}) collective-permute-start(bf16[3,128,512]{2,1,0:T(8,128)(2,1)} %collective-permute-done.57.rest_4_), channel_id=1, source_target_pairs={{0,8},{8,16},{16,24},{24,28},{28,20},{20,12},{12,4},{4,0},{1,9},{9... | collective-permute-start | bytes 1179656 | tf_op jit(solution)/shard_map/ppermute | solution.py:622
  73.8 41.7 %collective-permute-start.16 = (bf16[3,128,512]{2,1,0:T(8,128)(2,1)}, bf16[3,128,512]{2,1,0:T(8,128)(2,1)}, u32[]{:S(2)}, u32[]{:S(2)}) collective-permute-start(bf16[3,128,512]{2,1,0:T(8,128)(2,1)} %collective-permute-done.15.rest_0_), channel_id=1, source_target_pairs={{0,8},{8,16},{16,24},{24,28},{28,20},{20,12},{12,4},{4,0},{1,9},{9... | collective-permute-start | bytes 1179656 | tf_op jit(solution)/shard_map/ppermute | solution.py:622
  75.8 43.5 %collective-permute-start.29 = (bf16[3,128,512]{2,1,0:T(8,128)(2,1)}, bf16[3,128,512]{2,1,0:T(8,128)(2,1)}, u32[]{:S(2)}, u32[]{:S(2)}) collective-permute-start(bf16[3,128,512]{2,1,0:T(8,128)(2,1)} %collective-permute-done.28.rest_4_), channel_id=1, source_target_pairs={{8,0},{16,8},{24,16},{28,24},{20,28},{12,20},{4,12},{0,4},{9,1},{1... | collective-permute-start | bytes 1179656 | tf_op jit(solution)/shard_map/ppermute | solution.py:622
  75.8 48.6 %collective-permute-start.49 = (bf16[3,128,512]{2,1,0:T(8,128)(2,1)}, bf16[3,128,512]{2,1,0:T(8,128)(2,1)}, u32[]{:S(2)}, u32[]{:S(2)}) collective-permute-start(bf16[3,128,512]{2,1,0:T(8,128)(2,1)} %collective-permute-done.48.rest_0_), channel_id=1, source_target_pairs={{8,0},{16,8},{24,16},{28,24},{20,28},{12,20},{4,12},{0,4},{9,1},{1... | collective-permute-start | bytes 1179656 | tf_op jit(solution)/shard_map/ppermute | solution.py:622
  113.6 59.6 %collective-permute-start.24 = (bf16[3,128,512]{2,1,0:T(8,128)(2,1)}, bf16[3,128,512]{2,1,0:T(8,128)(2,1)S(1)}, u32[]{:S(2)}, u32[]{:S(2)}) collective-permute-start(bf16[3,128,512]{2,1,0:T(8,128)(2,1)} %get-tuple-element.47.refs_14_.refs_0_.rest_3_), channel_id=1, source_target_pairs={{0,8},{8,16},{16,24},{24,28},{28,20},{20,12},{12,4},{4,0},{1,9},{9... | collective-permute-start | bytes 1179656 | tf_op jit(solution)/shard_map/ppermute | solution.py:622
  115.4 58.3 %collective-permute-start.63 = (bf16[3,128,512]{2,1,0:T(8,128)(2,1)}, bf16[3,128,512]{2,1,0:T(8,128)(2,1)}, u32[]{:S(2)}, u32[]{:S(2)}) collective-permute-start(bf16[3,128,512]{2,1,0:T(8,128)(2,1)} %get-tuple-element.48.refs_15_.refs_1_.rest_7_), channel_id=1, source_target_pairs={{0,8},{8,16},{16,24},{24,28},{28,20},{20,12},{12,4},{4,0},{1,9},{9... | collective-permute-start | bytes 1179656 | tf_op jit(solution)/shard_map/ppermute | solution.py:622
  117.0 58.4 %collective-permute-start.61 = (bf16[3,128,512]{2,1,0:T(8,128)(2,1)}, bf16[3,128,512]{2,1,0:T(8,128)(2,1)}, u32[]{:S(2)}, u32[]{:S(2)}) collective-permute-start(bf16[3,128,512]{2,1,0:T(8,128)(2,1)} %get-tuple-element.46.refs_5_.refs_13_.refs_1_.rest_6_), channel_id=1, source_target_pairs={{0,8},{8,16},{16,24},{24,28},{28,20},{20,12},{12,4},{4,0},{1,9},{9... | collective-permute-start | bytes 1179656 | tf_op jit(solution)/shard_map/ppermute | solution.py:622
  122.9 54.4 %collective-permute-start.21 = (bf16[3,128,512]{2,1,0:T(8,128)(2,1)}, bf16[3,128,512]{2,1,0:T(8,128)(2,1)}, u32[]{:S(2)}, u32[]{:S(2)}) collective-permute-start(bf16[3,128,512]{2,1,0:T(8,128)(2,1)} %get-tuple-element.45.refs_12_.refs_0_.rest_2_), channel_id=1, source_target_pairs={{0,8},{8,16},{16,24},{24,28},{28,20},{20,12},{12,4},{4,0},{1,9},{9... | collective-permute-start | bytes 1179656 | tf_op jit(solution)/shard_map/ppermute | solution.py:622
  124.4 27.1 %collective-permute-start.10 = (f32[8,128]{1,0:T(8,128)S(1)}, f32[8,128]{1,0:T(8,128)S(1)}, u32[]{:S(2)}, u32[]{:S(2)}) collective-permute-start(f32[8,128]{1,0:T(8,128)S(1)} %add.61), channel_id=1, source_target_pairs={{0,12},{4,8},{8,4},{12,0},{16,28},{20,24},{24,20},{28,16},{1,13},{... | collective-permute-start | bytes 12296 | tf_op jit(solution)/shard_map/ppermute | solution.py:587
  183.0 28.2 %collective-permute-start.52 = (bf16[3,128,512]{2,1,0:T(8,128)(2,1)}, bf16[3,128,512]{2,1,0:T(8,128)(2,1)S(1)}, u32[]{:S(2)}, u32[]{:S(2)}) collective-permute-start(bf16[3,128,512]{2,1,0:T(8,128)(2,1)} %get-tuple-element.45.refs_12_.refs_0_.rest_2_), channel_id=1, source_target_pairs={{8,0},{16,8},{24,16},{28,24},{20,28},{12,20},{4,12},{0,4},{9,1},{1... | collective-permute-start | bytes 1179656 | tf_op jit(solution)/shard_map/ppermute | solution.py:622
  187.3 32.4 %collective-permute-start.31 = (bf16[3,128,512]{2,1,0:T(8,128)(2,1)}, bf16[3,128,512]{2,1,0:T(8,128)(2,1)S(1)}, u32[]{:S(2)}, u32[]{:S(2)}) collective-permute-start(bf16[3,128,512]{2,1,0:T(8,128)(2,1)} %get-tuple-element.44.refs_5_.refs_11_.refs_3_.rest_5_), channel_id=1, source_target_pairs={{8,0},{16,8},{24,16},{28,24},{20,28},{12,20},{4,12},{0,4},{9,1},{1... | collective-permute-start | bytes 1179656 | tf_op jit(solution)/shard_map/ppermute | solution.py:622
  187.9 37.8 %collective-permute-start.50 = (bf16[3,128,512]{2,1,0:T(8,128)(2,1)}, bf16[3,128,512]{2,1,0:T(8,128)(2,1)S(1)}, u32[]{:S(2)}, u32[]{:S(2)}) collective-permute-start(bf16[3,128,512]{2,1,0:T(8,128)(2,1)} %get-tuple-element.43.refs_10_.refs_2_.rest_1_), channel_id=1, source_target_pairs={{8,0},{16,8},{24,16},{28,24},{20,28},{12,20},{4,12},{0,4},{9,1},{1... | collective-permute-start | bytes 1179656 | tf_op jit(solution)/shard_map/ppermute | solution.py:622
  194.4 35.6 %collective-permute-start.30 = (bf16[3,128,512]{2,1,0:T(8,128)(2,1)}, bf16[3,128,512]{2,1,0:T(8,128)(2,1)}, u32[]{:S(2)}, u32[]{:S(2)}) collective-permute-start(bf16[3,128,512]{2,1,0:T(8,128)(2,1)} %collective-permute-done.29.rest_4_), channel_id=1, source_target_pairs={{8,0},{16,8},{24,16},{28,24},{20,28},{12,20},{4,12},{0,4},{9,1},{1... | collective-permute-start | bytes 1179656 | tf_op jit(solution)/shard_map/ppermute | solution.py:622
  202.8 29.6 %collective-permute-start.25 = (bf16[3,128,512]{2,1,0:T(8,128)(2,1)S(1)}, bf16[3,128,512]{2,1,0:T(8,128)(2,1)S(1)}, u32[]{:S(2)}, u32[]{:S(2)}) collective-permute-start(bf16[3,128,512]{2,1,0:T(8,128)(2,1)S(1)} %collective-permute-done.24.rest_3_), channel_id=1, source_target_pairs={{0,8},{8,16},{16,24},{24,28},{28,20},{20,12},{12,4},{4,0},{1,9},{9... | collective-permute-start | bytes 1179656 | tf_op jit(solution)/shard_map/ppermute | solution.py:622
  211.3 32.2 %collective-permute-start.64 = (bf16[3,128,512]{2,1,0:T(8,128)(2,1)}, bf16[3,128,512]{2,1,0:T(8,128)(2,1)}, u32[]{:S(2)}, u32[]{:S(2)}) collective-permute-start(bf16[3,128,512]{2,1,0:T(8,128)(2,1)} %collective-permute-done.63.rest_7_), channel_id=1, source_target_pairs={{0,8},{8,16},{16,24},{24,28},{28,20},{20,12},{12,4},{4,0},{1,9},{9... | collective-permute-start | bytes 1179656 | tf_op jit(solution)/shard_map/ppermute | solution.py:622
  245.0 31.7 %collective-permute-start.53 = (bf16[3,128,512]{2,1,0:T(8,128)(2,1)}, bf16[3,128,512]{2,1,0:T(8,128)(2,1)}, u32[]{:S(2)}, u32[]{:S(2)}) collective-permute-start(bf16[3,128,512]{2,1,0:T(8,128)(2,1)} %copy-done.5), channel_id=1, source_target_pairs={{8,0},{16,8},{24,16},{28,24},{20,28},{12,20},{4,12},{0,4},{9,1},{1... | collective-permute-start | bytes 1179656 | tf_op jit(solution)/shard_map/ppermute | solution.py:622
  254.6 38.9 %collective-permute-start.41 = (bf16[128,3072]{1,0:T(8,128)(2,1)}, bf16[128,3072]{1,0:T(8,128)(2,1)}, u32[]{:S(2)}, u32[]{:S(2)}) collective-permute-start(bf16[128,3072]{1,0:T(8,128)(2,1)} %get-tuple-element.55), channel_id=1, source_target_pairs={{0,1},{1,0},{2,3},{3,2},{4,5},{5,4},{6,7},{7,6},{8,9},{9,8},{10,11... | collective-permute-start | bytes 2359304 | tf_op jit(solution)/shard_map/ppermute | solution.py:587
  263.1 30.4 %collective-permute-start.43 = (bf16[128,3072]{1,0:T(8,128)(2,1)}, bf16[128,3072]{1,0:T(8,128)(2,1)}, u32[]{:S(2)}, u32[]{:S(2)}) collective-permute-start(bf16[128,3072]{1,0:T(8,128)(2,1)} %rows.5), channel_id=1, source_target_pairs={{0,3},{1,2},{2,1},{3,0},{4,7},{5,6},{6,5},{7,4},{8,11},{9,10},{10,... | collective-permute-start | bytes 2359304 | tf_op jit(solution)/shard_map/ppermute | solution.py:587
  264.7 35.4 %collective-permute-start.42 = (bf16[128,3072]{1,0:T(8,128)(2,1)}, bf16[128,3072]{1,0:T(8,128)(2,1)}, u32[]{:S(2)}, u32[]{:S(2)}) collective-permute-start(bf16[128,3072]{1,0:T(8,128)(2,1)} %rows.4), channel_id=1, source_target_pairs={{0,2},{1,3},{2,0},{3,1},{4,6},{5,7},{6,4},{7,5},{8,10},{9,11},{10,... | collective-permute-start | bytes 2359304 | tf_op jit(solution)/shard_map/ppermute | solution.py:587
  293.5 29.1 %collective-permute-start.33 = (bf16[3,128,512]{2,1,0:T(8,128)(2,1)}, bf16[3,128,512]{2,1,0:T(8,128)(2,1)}, u32[]{:S(2)}, u32[]{:S(2)}) collective-permute-start(bf16[3,128,512]{2,1,0:T(8,128)(2,1)} %collective-permute-done.32.rest_5_), channel_id=1, source_target_pairs={{8,0},{16,8},{24,16},{28,24},{20,28},{12,20},{4,12},{0,4},{9,1},{1... | collective-permute-start | bytes 1179656 | tf_op jit(solution)/shard_map/ppermute | solution.py:622
  293.5 34.5 %collective-permute-start.17 = (bf16[3,128,512]{2,1,0:T(8,128)(2,1)}, bf16[3,128,512]{2,1,0:T(8,128)(2,1)}, u32[]{:S(2)}, u32[]{:S(2)}) collective-permute-start(bf16[3,128,512]{2,1,0:T(8,128)(2,1)} %collective-permute-done.16.rest_0_), channel_id=1, source_target_pairs={{0,8},{8,16},{16,24},{24,28},{28,20},{20,12},{12,4},{4,0},{1,9},{9... | collective-permute-start | bytes 1179656 | tf_op jit(solution)/shard_map/ppermute | solution.py:622
  300.1 28.1 %collective-permute-start.26 = (bf16[3,128,512]{2,1,0:T(8,128)(2,1)}, bf16[3,128,512]{2,1,0:T(8,128)(2,1)}, u32[]{:S(2)}, u32[]{:S(2)}) collective-permute-start(bf16[3,128,512]{2,1,0:T(8,128)(2,1)} %copy-done.8), channel_id=1, source_target_pairs={{0,8},{8,16},{16,24},{24,28},{28,20},{20,12},{12,4},{4,0},{1,9},{9... | collective-permute-start | bytes 1179656 | tf_op jit(solution)/shard_map/ppermute | solution.py:622
  322.6 49.7 %collective-permute-start.44 = (bf16[4,384,256]{2,1,0:T(8,128)(2,1)}, bf16[4,384,256]{2,1,0:T(8,128)(2,1)}, u32[]{:S(2)}, u32[]{:S(2)}) collective-permute-start(bf16[4,384,256]{2,1,0:T(8,128)(2,1)} %get-tuple-element.61), channel_id=1, source_target_pairs={{0,4},{4,0},{8,12},{12,8},{16,20},{20,16},{24,28},{28,24},{1,5},{5... | collective-permute-start | bytes 2359304 | tf_op jit(solution)/shard_map/ppermute | solution.py:587
  328.2 47.8 %collective-permute-start.65 = (bf16[3,384,512]{2,1,0:T(8,128)(2,1)}, bf16[3,384,512]{2,1,0:T(8,128)(2,1)}, u32[]{:S(2)}, u32[]{:S(2)}) collective-permute-start(bf16[3,384,512]{2,1,0:T(8,128)(2,1)} %give.7), channel_id=1, source_target_pairs={{0,8},{8,16},{16,24},{24,28},{28,20},{20,12},{12,4},{4,0},{1,9},{9... | collective-permute-start | bytes 3538952 | tf_op jit(solution)/shard_map/ppermute | solution.py:622
  330.2 48.5 %collective-permute-start.56 = (bf16[3,384,512]{2,1,0:T(8,128)(2,1)}, bf16[3,384,512]{2,1,0:T(8,128)(2,1)}, u32[]{:S(2)}, u32[]{:S(2)}) collective-permute-start(bf16[3,384,512]{2,1,0:T(8,128)(2,1)} %give.6), channel_id=1, source_target_pairs={{8,0},{16,8},{24,16},{28,24},{20,28},{12,20},{4,12},{0,4},{9,1},{1... | collective-permute-start | bytes 3538952 | tf_op jit(solution)/shard_map/ppermute | solution.py:622
  346.2 49.6 %collective-permute-start.40 = (bf16[3,384,512]{2,1,0:T(8,128)(2,1)}, bf16[3,384,512]{2,1,0:T(8,128)(2,1)}, u32[]{:S(2)}, u32[]{:S(2)}) collective-permute-start(bf16[3,384,512]{2,1,0:T(8,128)(2,1)} %give.5), channel_id=1, source_target_pairs={{8,0},{16,8},{24,16},{28,24},{20,28},{12,20},{4,12},{0,4},{9,1},{1... | collective-permute-start | bytes 3538952 | tf_op jit(solution)/shard_map/ppermute | solution.py:622
  346.2 49.6 %collective-permute-start.27 = (bf16[3,384,512]{2,1,0:T(8,128)(2,1)}, bf16[3,384,512]{2,1,0:T(8,128)(2,1)}, u32[]{:S(2)}, u32[]{:S(2)}) collective-permute-start(bf16[3,384,512]{2,1,0:T(8,128)(2,1)} %give.4), channel_id=1, source_target_pairs={{0,8},{8,16},{16,24},{24,28},{28,20},{20,12},{12,4},{4,0},{1,9},{9... | collective-permute-start | bytes 3538952 | tf_op jit(solution)/shard_map/ppermute | solution.py:622
  (49 other events, 922.5 us)
